TPU v7x, 128 devices: a whole 4x4x4 slice. The times are simulated.
128 devices in a mesh: dp: 32 (over x, z, y_hi), mp: 4 (over y_lo, core).
Axes of the slice: x: 4, y: 4 (y_hi: 2, y_lo: 2; y = y_hi * 2 + y_lo), z: 4, core: 2. Of those that a mesh axis runs over, the one named last changes fastest.
Arguments:
- activations: bfloat16 [32768, 8192], P('dp', 'mp'), may hold values from -6 to 6
- cot_true: bfloat16 [32768, 1024], P('dp', 'mp'), may hold values from -6 to 6
- cot_sampled: bfloat16 [32768, 1024], P('dp', 'mp'), may hold values from -6 to 6
- tile_mask: int32 [64, 8], replicated, may hold values from 0 to 1, as said below
- moment: float32 [8192, 1024], P('dp', 'mp'), may hold values from -0.0012207031 to 0.0012207031
- curvature: float32 [8192, 1024], P('dp', 'mp'), may hold values from 0.003 to 3
Outputs:
- update: float32 [8192, 1024], P('dp', 'mp')
- new_curvature: float32 [8192, 1024], P('dp', 'mp')
Inputs may be any that keep to these rules, and one draw needn't show every extreme that they name: Every column of tile_mask holds exactly 16 ones.
All inputs are finite; a program needn't handle non-finite values.
Results may differ from a plain program's by a relative error of at most 0.0003.
Values may be sent and summed in bfloat16 or wider, within the bound.
A program may use at most 128 MiB of HBM per device.

v0:
```python
import jax
import jax.numpy as jnp
from jax import lax
from jax.sharding import PartitionSpec as P

D = 8192
BLOCK = 128


BETA_ONE = 0.965
BETA_TWO = 0.99
GAMMA_CLIP = 0.01
CONTRACT = (((0,), (0,)), ((), ()))


def expand_tiles(tile_grid, tile_width):
    return jnp.repeat(jnp.repeat(tile_grid, tile_width, axis=0), tile_width, axis=1).astype(
        jnp.float32
    )


def on_device(activations, cot_true, cot_sampled, tile_mask, moment, curvature):
    dp_count = lax.axis_size("dp")
    kv_cols = cot_true.shape[1]
    col_tiles = kv_cols // BLOCK
    row_count = D // dp_count
    tokens_all = activations.shape[0] * dp_count
    inv_tokens = 1.0 / tokens_all
    panel = lax.all_gather(activations, "mp", axis=1, tiled=True)
    cotangents = jnp.concatenate([cot_true, cot_sampled], axis=1)
    local_tiles = lax.dynamic_slice_in_dim(
        tile_mask, lax.axis_index("mp") * col_tiles, col_tiles, 1
    )
    owned_tiles = row_count // BLOCK
    first_tile = lax.axis_index("dp") * owned_tiles
    product = lax.dot_general(panel, cotangents, CONTRACT, preferred_element_type=jnp.float32)
    row_mask = expand_tiles(local_tiles, BLOCK)
    owned = lax.psum_scatter(
        product * inv_tokens * jnp.concatenate([row_mask, row_mask], axis=1),
        "dp",
        scatter_dimension=0,
        tiled=True,
    )
    owned_mask = expand_tiles(
        lax.dynamic_slice_in_dim(local_tiles, first_tile, owned_tiles, 0), BLOCK
    )
    grad_true = owned[:, :kv_cols]
    grad_sampled = owned[:, kv_cols:]
    moment_new = BETA_ONE * moment + (1.0 - BETA_ONE) * grad_true
    hessian = tokens_all * grad_sampled * grad_sampled
    curvature_next = BETA_TWO * curvature + (1.0 - BETA_TWO) * hessian
    update = jnp.clip(moment_new / (GAMMA_CLIP * curvature_next), -1.0, 1.0) * owned_mask
    return (update, curvature_next * owned_mask)


def solution(mesh):
    return jax.shard_map(
        on_device,
        mesh=mesh,
        in_specs=(P("dp", "mp"), P("dp", "mp"), P("dp", "mp"), P(), P("dp", "mp"), P("dp", "mp")),
        out_specs=(P("dp", "mp"), P("dp", "mp")),
        check_vma=False,
    )
```

profile of v0, /device:TPU:5, one launch (start us, length us, event | category | flops | bytes accessed | tf_op | source)
XLA Modules:
  0.0 552.3 jit_solution(4977731851931626802)
XLA Ops:
  7.2 0.0 all-gather.2.cloned.1.call-start
  7.2 0.7 all-gather.2.cloned.1.call-update
  7.9 0.0 reduce-scatter.2.cloned.1.call-start
  7.9 0.7 dynamic-slice_convert_fusion.1
  8.6 0.1 broadcast_bitcast_fusion
  8.7 0.1 copy.16
  8.8 154.7 %all-gather.2.cloned.1.call-done = bf16[1024,8192]{1,0:T(8,128)(2,1)} async-done(((bf16[1024,2048]{1,0:T(8,128)(2,1)}), bf16[1024,8192]{1,0:T(8,128)(2,1)}) %all-gather.2.cloned.1.call-update) | async-done | bytes 16777232 | tf_op jit(solution)/shard_map/all_gather | solution.py:29
  163.5 0.9 broadcast_in_dim.13
  164.5 16.2 %maximum_multiply_fusion = f32[8192,512]{0,1:T(8,128)} fusion(f32[8192,256]{0,1:T(8,128)S(1)} %bitcast.21, bf16[1024,8192]{1,0:T(8,128)(2,1)} %all-gather.2.cloned.1.call-done, bf16[1024,256]{1,0:T(8,128)(2,1)} %param.8, bf16[1024,256]{1,0:T(8,128)(2,1)} %param.7), kind=kOutput, calls=%fused_computation | convolution fusion | flops 8604614656 | bytes 42991616 | tf_op jit(solution)/shard_map/dot_general | solution.py:36
  180.6 0.0 copy-start
  180.6 0.0 copy-start.1
  180.6 0.0 reduce-scatter.2.cloned.1.call-update
  180.7 0.8 dynamic-slice_convert_fusion
  181.5 0.1 broadcast_bitcast_fusion.1
  181.6 0.0 copy-done
  181.6 0.1 copy.8
  181.7 0.0 copy-done.1
  181.7 0.1 copy.9
  181.9 360.8 %reduce-scatter.2.cloned.1.call-done = f32[256,512]{0,1:T(8,128)} async-done(((f32[8192,512]{0,1:T(8,128)}), f32[256,512]{0,1:T(8,128)}) %reduce-scatter.2.cloned.1.call-update) | async-done | bytes 524304 | tf_op jit(solution)/shard_map/reduce_scatter | solution.py:38
  542.6 1.2 bitcast_multiply_fusion
  543.8 0.8 copy.10
  544.6 0.8 copy.11
  (1 shorter events, 0.0 us)
Async XLA Ops:
  7.2 156.4 %all-gather.2.cloned.1.call-start = ((), (), s32[]{:S(2)}) async-start(), calls=%async_computation.1 | async-start | bytes 20971520 | tf_op jit(solution)/shard_map/all_gather | solution.py:29
  7.9 534.7 %reduce-scatter.2.cloned.1.call-start = ((), (), s32[]{:S(2)}) async-start(), calls=%async_computation.2 | async-start | bytes 17301504 | tf_op jit(solution)/shard_map/reduce_scatter | solution.py:38
  180.6 0.9 copy-start
  180.6 1.1 copy-start.1
Sparse Core Ops, SparseCore 0:
  9.6 153.8 all-gather.1
  180.8 361.8 reduce-scatter.1
where the time goes:
time: 554 us; the launch traced here: 552 us
  waiting for transfers between devices  516 us (93%)
  matrix products  16.2 us (3%)
  between operations  14.1 us (3%)
    reduce_scatter x1, waiting for transfers between devices, on_device(): lax.psum_scatter(product * inv_tokens * jnp.concatenate([row_mask, row_ma...  361 us
    all_gather x1, waiting for transfers between devices, on_device(): panel = lax.all_gather(activations, 'mp', axis=1, tiled=True)  155 us
    dot_general x1, matrix products, on_device(): lax.dot_general(panel, cotangents, CONTRACT, preferred_element_type=jnp.f...  16.2 us
  transfers between devices with their start and end apart: 2, of which 2 were waited for; matrix products, arithmetic and copies ran while one was open for 0% of the time, Pallas kernels for 0%

commit v1 on v0

v1 whole, which is shorter than its diff:
```python
import functools

import jax
import jax.numpy as jnp
from jax import lax
from jax.experimental import pallas as pl
from jax.experimental.pallas import tpu as pltpu
from jax.sharding import PartitionSpec as P

D = 8192
BLOCK = 128
TOKENS = 32768

BETA_ONE = 0.965
BETA_TWO = 0.99
GAMMA_CLIP = 0.01
CONTRACT = (((0,), (0,)), ((), ()))
MESH = pl.DeviceIdType.MESH

SG = 26
HALF = SG // 2
TILE_ROWS = 16


def device_at(x, z, h, m):
    return (x * 8 + z * 2 + h, m)


def remote(src, dst, send_sem, recv_sem, device):
    return pltpu.make_async_remote_copy(
        src_ref=src, dst_ref=dst, send_sem=send_sem, recv_sem=recv_sem,
        device_id=device, device_id_type=MESH,
    )


def kernel(
    row_ref, col_ref, place_ref, acts_ref, true_ref, sampled_ref, out_ref,
    acts_t, near_cots, far_cots, part, relay1, final1, relay2, final2, mid, last, over_h, tiles, dense, landed,
    local_sem, pair_send, pair_recv, far_send, far_recv, fwd_send, fwd_recv,
    ring_send, ring_recv, h_send, h_recv, out_send, out_recv,
):
    dp = lax.axis_index("dp")
    m = lax.axis_index("mp")
    x, z, h = dp // 8, lax.rem(dp // 2, 4), lax.rem(dp, 2)
    l, core = m // 2, lax.rem(m, 2)
    pair = device_at(x, z, h, l * 2 + 1 - core)
    far = device_at(x, z, h, (1 - l) * 2 + core)
    up_x, down_x = lax.rem(x + 1, 4), lax.rem(x + 3, 4)
    up_z, down_z = lax.rem(z + 1, 4), lax.rem(z + 3, 4)
    along_x = (device_at(up_x, z, h, m), device_at(down_x, z, h, m))
    along_z = (device_at(x, up_z, h, m), device_at(x, down_z, h, m))
    across_h = device_at(x, z, 1 - h, m)

    barrier = pltpu.get_barrier_semaphore()
    for other in (pair, far, *along_x, *along_z, across_h):
        pl.semaphore_signal(barrier, inc=1, device_id=other, device_id_type=MESH)

    def greet(source, carry):
        @pl.when(jnp.logical_not(jnp.logical_and(source == dp, m == x)))
        def _():
            pl.semaphore_signal(barrier, inc=1, device_id=(source, x), device_id_type=MESH)
        return carry

    lax.fori_loop(0, 32, greet, 0)
    pl.semaphore_wait(barrier, jnp.where(m == x, 38, 39))

    def own(cc, g):
        return (true_ref, sampled_ref)[g].at[:, pl.ds(cc * BLOCK, BLOCK)]

    def place_of(cots, owner_core, cc, g):
        return cots.at[owner_core * 2 + cc, :, pl.ds(g * BLOCK, BLOCK)]

    pieces = [(cc, g) for cc in range(2) for g in range(2)]
    locals_, pairs, fars, fwds = [], [], [], []
    for i, (cc, g) in enumerate(pieces):
        here, there = place_of(near_cots, core, cc, g), place_of(far_cots, core, cc, g)
        fars.append(remote(own(cc, g), there, far_send.at[i], far_recv.at[i], far))
        pairs.append(remote(own(cc, g), here, pair_send.at[i], pair_recv.at[i], pair))
        locals_.append(pltpu.make_async_copy(own(cc, g), here, local_sem.at[i]))
    for copy in (*fars, *pairs, *locals_):
        copy.start()

    def transpose(r, carry):
        acts_t[r] = acts_ref[:, pl.ds(pl.multiple_of(r * BLOCK, BLOCK), BLOCK)].T
        return carry

    lax.fori_loop(0, TILE_ROWS, transpose, 0)

    def products(group):
        cots = (near_cots, far_cots)[group]

        def one(i, carry):
            for u in range(2):
                s = 2 * i + u
                row, col = row_ref[group * SG + s], col_ref[group * SG + s]
                tile = jnp.dot(acts_t[row], cots[col], preferred_element_type=jnp.float32)
                for g in range(2):
                    part[group, g, :, s] = tile[:, g * BLOCK : (g + 1) * BLOCK].reshape(16, 8, BLOCK)
            return carry

        lax.fori_loop(0, SG // 2, one, 0)

    def ring_open(ids, pos, neighbours, chunk, relay, final):
        send, recv = ring_send.at[ids], ring_recv.at[ids]
        up, down = neighbours
        opposite = lax.rem(pos + 2, 4)
        nxt, prv = lax.rem(pos + 1, 4), lax.rem(pos + 3, 4)
        copies = [
            remote(chunk(opposite, 0), relay.at[0], send.at[0], recv.at[0], up),
            remote(chunk(opposite, 1), relay.at[1], send.at[1], recv.at[1], down),
            remote(chunk(nxt, 1), final.at[0], send.at[2], recv.at[2], up),
            remote(chunk(prv, 0), final.at[1], send.at[3], recv.at[3], down),
            remote(relay.at[0], final.at[2], send.at[4], recv.at[4], up),
            remote(relay.at[1], final.at[3], send.at[5], recv.at[5], down),
        ]
        for copy in copies[:4]:
            copy.start()
        return copies

    def ring_turn(copies, pos, chunk, relay, add):
        nxt, prv = lax.rem(pos + 1, 4), lax.rem(pos + 3, 4)
        copies[0].wait_recv()
        add(relay.at[0], (relay.at[0], chunk(nxt, 0)))
        copies[4].start()
        copies[1].wait_recv()
        add(relay.at[1], (relay.at[1], chunk(prv, 1)))
        copies[5].start()

    def ring_close(copies, pos, chunk, final, add, result):
        for copy in copies[2:]:
            copy.wait_recv()
        add(result(0), (chunk(pos, 0), final.at[1], final.at[2]))
        add(result(1), (chunk(pos, 1), final.at[0], final.at[3]))

    def add_big(dst, srcs):
        for i in range(2):
            total = srcs[0][i] + srcs[1][i]
            for src in srcs[2:]:
                total = total + src[i]
            dst[i] = total

    def add_small(dst, srcs):
        total = srcs[0][...] + srcs[1][...]
        for src in srcs[2:]:
            total = total + src[...]
        dst[...] = total

    started = []

    def reduce_group(group):
        streams = ((x, along_x, z, along_z), (z, along_z, x, along_x))

        def chunk1(g):
            return lambda p, half: part.at[group, g, pl.ds(p * 4 + half * 2, 2)]

        def chunk2(g):
            return lambda p, half: mid.at[group, g, p, pl.ds(half * HALF, HALF)]

        first = []
        for g, (pos, near, _, _) in enumerate(streams):
            first.append(ring_open((group, g, 0), pos, near, chunk1(g), relay1.at[group, g], final1.at[group, g]))
        for g, (pos, _, _, _) in enumerate(streams):
            ring_turn(first[g], pos, chunk1(g), relay1.at[group, g], add_big)
        second = []
        for g, (pos, _, pos2, near2) in enumerate(streams):
            ring_close(
                first[g], pos, chunk1(g), final1.at[group, g], add_big,
                lambda half: mid.at[group, g, pl.ds(half * 2, 2)],
            )
            second.append(ring_open((group, g, 1), pos2, near2, chunk2(g), relay2.at[group, g], final2.at[group, g]))
        for g, (_, _, pos2, _) in enumerate(streams):
            ring_turn(second[g], pos2, chunk2(g), relay2.at[group, g], add_small)
        for g, (_, _, pos2, _) in enumerate(streams):
            ring_close(
                second[g], pos2, chunk2(g), final2.at[group, g], add_small,
                lambda half: last.at[group, g, pl.ds(half * HALF, HALF)],
            )
        swap = remote(
            last.at[group, 1 - h], over_h.at[group], h_send.at[group], h_recv.at[group], across_h
        )
        swap.start()
        for copies in (*first, *second):
            started.extend(copies)
        started.append(swap)
        swap.wait_recv()
        tiles[group, pl.ds(0, SG)] = last[group, h] + over_h[group]
        tiles[group, SG] = jnp.zeros((8, BLOCK), jnp.float32)

        columns = l if group == 0 else 1 - l

        def deliver(t, carry):
            for q in range(4):
                lo, cc = q // 2, q % 2
                row = (t // 2) * 2 + lo
                at = place_ref[group * 64 + row * 4 + lax.rem(t, 2) * 2 + cc]
                dense[group, t, q] = tiles[group, at]
            return carry

        lax.fori_loop(0, 16, deliver, 0)

        def owner(t):
            return m * 8 + t // 2, columns * 2 + lax.rem(t, 2)

        def itself(t):
            return jnp.logical_and(owner(t)[0] == dp, owner(t)[1] == m)

        def outgoing(t):
            return remote(dense.at[group, t], landed.at[dp], out_send.at[group, t], out_recv.at[dp], owner(t))

        def send(t, carry):
            @pl.when(itself(t))
            def _():
                pltpu.make_async_copy(dense.at[group, t], landed.at[dp], out_recv.at[dp]).start()

            @pl.when(jnp.logical_not(itself(t)))
            def _():
                outgoing(t).start()

            return carry

        def drain(t, carry):
            @pl.when(jnp.logical_not(itself(t)))
            def _():
                outgoing(t).wait_send()

            return carry

        lax.fori_loop(0, 16, send, 0)
        return drain

    for copy in (*locals_,):
        copy.wait()
    for copy in pairs:
        copy.wait_recv()
    products(0)
    drain0 = reduce_group(0)
    for i, (cc, g) in enumerate(pieces):
        fars[i].wait_recv()
        there = place_of(far_cots, core, cc, g)
        fwd = remote(there, there, fwd_send.at[i], fwd_recv.at[i], pair)
        fwd.start()
        fwds.append(fwd)
    for copy in fwds:
        copy.wait_recv()
    products(1)
    drain1 = reduce_group(1)

    def arrive(source, carry):
        pltpu.make_async_copy(landed.at[source], landed.at[source], out_recv.at[source]).wait()
        for q in range(4):
            lo, cc = q // 2, q % 2
            gx, gz, gh = source // 8, lax.rem(source // 2, 4), lax.rem(source, 2)
            strip = jnp.where(gh == 0, gx * 4 + gz, gz * 4 + gx)
            out_ref[
                gh, pl.ds(pl.multiple_of(lo * BLOCK + strip * 8, 8), 8), pl.ds(cc * BLOCK, BLOCK)
            ] = landed[source, q]
        return carry

    lax.fori_loop(0, 32, arrive, 0)

    for copy in (*fars, *pairs, *fwds, *started):
        copy.wait_send()
    lax.fori_loop(0, 16, drain0, 0)
    lax.fori_loop(0, 16, drain1, 0)


def reduced_tiles(rows, cols, places, activations, cot_true, cot_sampled):
    f32, bf16 = jnp.float32, jnp.bfloat16
    dma = pltpu.SemaphoreType.DMA
    vmem = pl.BlockSpec(memory_space=pltpu.VMEM)
    smem = pl.BlockSpec(memory_space=pltpu.SMEM)
    tokens = activations.shape[0]
    return pl.pallas_call(
        kernel,
        out_shape=jax.ShapeDtypeStruct((2, 2 * BLOCK, 2 * BLOCK), f32),
        in_specs=[smem, smem, smem, vmem, vmem, vmem],
        out_specs=vmem,
        scratch_shapes=[
            pltpu.VMEM((TILE_ROWS, BLOCK, tokens), bf16),
            pltpu.VMEM((4, tokens, 2 * BLOCK), bf16),
            pltpu.VMEM((4, tokens, 2 * BLOCK), bf16),
            pltpu.VMEM((2, 2, 16, SG, 8, BLOCK), f32),
            pltpu.VMEM((2, 2, 2, 2, SG, 8, BLOCK), f32),
            pltpu.VMEM((2, 2, 4, 2, SG, 8, BLOCK), f32),
            pltpu.VMEM((2, 2, 2, HALF, 8, BLOCK), f32),
            pltpu.VMEM((2, 2, 4, HALF, 8, BLOCK), f32),
            pltpu.VMEM((2, 2, 4, SG, 8, BLOCK), f32),
            pltpu.VMEM((2, 2, SG, 8, BLOCK), f32),
            pltpu.VMEM((2, SG, 8, BLOCK), f32),
            pltpu.VMEM((2, SG + 1, 8, BLOCK), f32),
            pltpu.VMEM((2, 16, 4, 8, BLOCK), f32),
            pltpu.VMEM((32, 4, 8, BLOCK), f32),
            dma((4,)), dma((4,)), dma((4,)), dma((4,)), dma((4,)), dma((4,)), dma((4,)),
            dma((2, 2, 2, 6)), dma((2, 2, 2, 6)), dma((2,)), dma((2,)), dma((2, 16)), dma((32,)),
        ],
        compiler_params=pltpu.CompilerParams(
            collective_id=0, has_side_effects=True, vmem_limit_bytes=60 << 20
        ),
        name="reduced_tiles",
    )(rows, cols, places, activations, cot_true, cot_sampled)


def tables(tile_mask, m, round_):
    own_rows = lax.dynamic_slice_in_dim(tile_mask, m * TILE_ROWS, TILE_ROWS, 0)
    halves = own_rows.reshape(TILE_ROWS, 2, 4)
    halves = jnp.where(m < 2, halves, halves[:, ::-1])
    kept = halves.transpose(1, 0, 2).reshape(2, 64) > 0
    index = jnp.arange(64)
    before = jnp.sum(kept[:, None, :] & (index[None, :] < index[:, None])[None], axis=2)
    slot = before - round_ * SG
    here = kept & (slot >= 0) & (slot < SG)
    places = jnp.where(here, slot, SG).astype(jnp.int32).reshape(-1)
    chosen = here[:, None, :] & (slot[:, None, :] == jnp.arange(SG)[None, :, None])
    def listed(values):
        return jnp.sum(jnp.where(chosen, values[:, None, :], 0), axis=2).astype(jnp.int32).reshape(-1)

    rows, cols = listed((index // 4)[None, :]), listed((index % 4)[None, :])
    return rows, cols, places


def on_device(activations, cot_true, cot_sampled, tile_mask, moment, curvature):
    m = lax.axis_index("mp")
    dp = lax.axis_index("dp")
    tokens_all = activations.shape[0] * lax.axis_size("dp")
    counts = jnp.sum(tile_mask.reshape(4, TILE_ROWS, 2, 4) > 0, axis=(1, 3))
    rounds = (jnp.max(counts) + SG - 1) // SG

    def step(state):
        round_, total = state
        rows, cols, places = tables(tile_mask, m, round_)
        return round_ + 1, total + reduced_tiles(rows, cols, places, activations, cot_true, cot_sampled)

    start = (jnp.int32(0), jnp.zeros((2, 2 * BLOCK, 2 * BLOCK), jnp.float32))
    _, sums = lax.while_loop(lambda state: state[0] < rounds, step, start)
    owned = lax.dynamic_slice(tile_mask, (dp * 2, m * 2), (2, 2))
    owned_mask = jnp.repeat(jnp.repeat(owned, BLOCK, axis=0), BLOCK, axis=1).astype(jnp.float32)
    grads = sums * (1.0 / tokens_all)
    moment_new = BETA_ONE * moment + (1.0 - BETA_ONE) * grads[0]
    hessian = tokens_all * grads[1] * grads[1]
    curvature_next = BETA_TWO * curvature + (1.0 - BETA_TWO) * hessian
    update = jnp.clip(moment_new / (GAMMA_CLIP * curvature_next), -1.0, 1.0) * owned_mask
    return (update, curvature_next * owned_mask)


def solution(mesh):
    return jax.shard_map(
        on_device,
        mesh=mesh,
        in_specs=(P("dp", "mp"), P("dp", "mp"), P("dp", "mp"), P(), P("dp", "mp"), P("dp", "mp")),
        out_specs=(P("dp", "mp"), P("dp", "mp")),
        check_vma=False,
    )
```

time: 554 us -> 104 us (0.19)
  waiting for transfers between devices: 516 us -> 0 us
  Pallas kernels: 0 us -> 92.8 us
  matrix products: 16.2 us -> 0 us
  between operations: 14.1 us -> 1.38 us
    reduce_scatter x1 -> x0, waiting for transfers between devices: 361 us -> none  [on_device(): lax.psum_scatter(product * inv_tokens * jnp.concatenate([row_mask, row_ma...]
    all_gather x1 -> x0, waiting for transfers between devices: 155 us -> none  [on_device(): panel = lax.all_gather(activations, 'mp', axis=1, tiled=True)]
    pallas_call x0 -> x1, Pallas kernels: none -> 92.8 us  [reduced_tiles(): pl.pallas_call(kernel, out_shape=jax.ShapeDtypeStruct((2, 2 * BLOCK, 2 *...]
    dot_general x1 -> x0, matrix products: 16.2 us -> none  [on_device(): lax.dot_general(panel, cotangents, CONTRACT, preferred_element_type=jnp.f...]
  transfers between devices with their start and end apart: 2 -> 0, of which waited for: 2 -> 0; matrix products, arithmetic and copies ran while one was open for 0% -> 0% of each run, Pallas kernels for 0% -> 0%
where the time goes in v1:
time: 104 us; the launch traced here: 103 us
  Pallas kernels  92.8 us (89%)
  other arithmetic  5.98 us (6%)
  local copies, waits for them, and re-layouts  3.15 us (3%)
  between operations  1.38 us (1%)
    pallas_call x1, Pallas kernels, reduced_tiles(): pl.pallas_call(kernel, out_shape=jax.ShapeDtypeStruct((2, 2 * BLOCK, 2 *...  92.8 us

profile of v1, /device:TPU:5, one launch (start us, length us, event | category | flops | bytes accessed | tf_op | source)
XLA Modules:
  0.0 103.4 jit_solution(7229488097135422213)
XLA Ops:
  0.6 0.8 constant_dynamic-slice_fusion
  1.4 0.7 compare_convert_fusion
  2.1 0.1 reshape.102
  2.2 0.1 reduce_sum.45
  2.3 0.6 reduce_max.9
  3.7 0.0 copy-start
  3.7 0.0 copy-start.1
  3.7 97.5 %while.12 = (s32[]{:T(128)}, f32[2,256,256]{2,1,0:T(8,128)S(1)}, s32[]{:T(128)}, pred[]{:T(512)}, s32[16,8]{0,1:T(8,128)S(1)}, /*index=5*/bf16[1024,2048]{1,0:T(...) while((s32[]{:T(128)}, f32[2,256,256]{2,1,0:T(8,128)S(1)}, ...), condition=%wide.region_6.7_spmd, body=%wide.region_2.6_spmd.sunk | while | flops 181787 | bytes 1590422 | solution.py:334
  3.7 0.1 copy.28
  3.8 0.1 gt.48
  3.9 0.1 convert_reduce_fusion.2
  4.1 1.0 select_reduce_fusion.3
  5.0 0.1 copy.29
  5.1 0.6 reshape.105.row_ref
  5.7 0.1 copy.30
  5.8 0.7 reshape.106.col_ref
  6.5 0.1 sub.47
  6.5 0.1 gt.49
  6.7 0.6 and_select_fusion.6.place_ref
  7.2 92.8 %reduced_tiles.4 = f32[2,256,256]{2,1,0:T(8,128)} custom-call(s32[52]{0:T(128)} %reshape.105.row_ref, s32[52]{0:T(128)} %reshape.106.col_ref, s32[128]{0:T(128)} %and_select_fusion.6.place_ref, bf16[1024,2048]{1,0:T(8,128)(2,1)} %get-tuple-element.226.acts_ref, bf16[1024,256]{1,0:T(8,128)(2,1)} %get-tuple-element.227.true_ref, ...), custom_call_target="tpu_custom_call" | custom-call | tf_op jit(solution)/shard_map/while/body/reduced_tiles/pallas_call | solution.py:273
  100.0 1.2 %add.78 = f32[2,256,256]{2,1,0:T(8,128)S(1)} add(f32[2,256,256]{2,1,0:T(8,128)S(1)} %get-tuple-element.212, f32[2,256,256]{2,1,0:T(8,128)} %reduced_tiles.4) | non-fusion elementwise | flops 131072 | bytes 1572864 | tf_op jit(solution)/shard_map/while/body/add | solution.py:331
  101.3 0.8 dynamic-slice_convert_fusion
  102.0 0.1 copy.21
  102.2 0.3 broadcast_in_dim.51
  102.5 0.0 copy-done
  102.5 0.0 copy-done.1
  102.5 0.9 bitcast_multiply_fusion
  (7 shorter events, 0.1 us)
Async XLA Ops:
  3.7 98.8 %copy-start = (f32[256,256]{1,0:T(8,128)S(1)}, f32[256,256]{1,0:T(8,128)}, u32[]{:S(2)}) copy-start(f32[256,256]{1,0:T(8,128)} %param.13) | copy-start | bytes 786436
  3.7 98.8 %copy-start.1 = (f32[256,256]{1,0:T(8,128)S(1)}, f32[256,256]{1,0:T(8,128)}, u32[]{:S(2)}) copy-start(f32[256,256]{1,0:T(8,128)} %param.12) | copy-start | bytes 786436

commit v2 on v0

v2 whole, which is shorter than its diff:
```python
import jax
import jax.numpy as jnp
from jax import lax
from jax.experimental import pallas as pl
from jax.experimental.pallas import tpu as pltpu
from jax.sharding import PartitionSpec as P

D = 8192
BLOCK = 128
BETA_ONE = 0.965
BETA_TWO = 0.99
GAMMA_CLIP = 0.01
MESH = pl.DeviceIdType.MESH
F32, BF16, I32 = jnp.float32, jnp.bfloat16, jnp.int32

GROUP_COLS = (4, 2, 2)
WAVES = ((0, 0, 14), (0, 14, 12), (1, 0, 16), (2, 0, 16))
GROUP_SLOTS = tuple(sum(n for g, _, n in WAVES if g == group) for group in range(3))
TILE_ROWS = 16

ROWS_AT, COLS_AT, PLACES_AT = [], [], []
TABLE_SIZE = 0
for _slots, _cols in zip(GROUP_SLOTS, GROUP_COLS):
    ROWS_AT.append(TABLE_SIZE)
    COLS_AT.append(TABLE_SIZE + _slots)
    PLACES_AT.append(TABLE_SIZE + 2 * _slots)
    TABLE_SIZE += 2 * _slots + TILE_ROWS * _cols


def remote(src, dst, send_sem, recv_sem, device):
    return pltpu.make_async_remote_copy(
        src_ref=src, dst_ref=dst, send_sem=send_sem, recv_sem=recv_sem,
        device_id=device, device_id_type=MESH,
    )


def scratch_list(tokens):
    dma = pltpu.SemaphoreType.DMA
    shapes = dict(
        acts=pltpu.VMEM((tokens, TILE_ROWS * BLOCK), BF16),
        acts_t=pltpu.VMEM((TILE_ROWS, BLOCK, tokens), BF16),
        landed=pltpu.VMEM((32, 2, 2, 8, BLOCK), F32),
        in_sem=dma((7,)),
        pair_send=dma((4,)), pair_recv=dma((4,)),
        far_send=dma((4,)), far_recv=dma((4,)),
        fwd_send=dma((4,)), fwd_recv=dma((4,)),
    )
    for g, cols in enumerate(GROUP_COLS):
        n = GROUP_SLOTS[g]
        shapes[f"cots{g}"] = pltpu.VMEM((cols, tokens, 2 * BLOCK), BF16)
        shapes[f"tiles{g}"] = pltpu.VMEM((n + 1, 8, BLOCK), F32)
        per_owner = (2, 2) if g == 0 else (2,)
        shapes[f"dense{g}"] = pltpu.VMEM((16, *per_owner, 8, BLOCK), F32)
        shapes[f"out_send{g}"] = dma((16,))
        shapes[f"out_recv{g}"] = dma((32,))
    for w, (_, _, n) in enumerate(WAVES):
        half = n // 2
        shapes[f"part{w}"] = pltpu.VMEM((2, 16, n, 8, BLOCK), F32)
        shapes[f"relay1_{w}"] = pltpu.VMEM((2, 2, 2, n, 8, BLOCK), F32)
        shapes[f"final1_{w}"] = pltpu.VMEM((2, 4, 2, n, 8, BLOCK), F32)
        shapes[f"relay2_{w}"] = pltpu.VMEM((2, 2, half, 8, BLOCK), F32)
        shapes[f"final2_{w}"] = pltpu.VMEM((2, 4, half, 8, BLOCK), F32)
        shapes[f"mid{w}"] = pltpu.VMEM((2, 4, n, 8, BLOCK), F32)
        shapes[f"last{w}"] = pltpu.VMEM((2, n, 8, BLOCK), F32)
        shapes[f"over{w}"] = pltpu.VMEM((n, 8, BLOCK), F32)
        shapes[f"ring_send{w}"] = dma((2, 2, 6))
        shapes[f"ring_recv{w}"] = dma((2, 2, 6))
        shapes[f"swap_send{w}"] = dma((1,))
        shapes[f"swap_recv{w}"] = dma((1,))
    return shapes


def kernel(*refs):
    refs = list(refs)
    names = list(scratch_list(8))
    r = dict(zip(names, refs[-len(names):]))
    table_ref, acts_hbm, true_ref, sampled_ref, out_ref = refs[: -len(names)]

    dp = lax.axis_index("dp")
    m = lax.axis_index("mp")
    x, z, h = dp // 8, lax.rem(dp // 2, 4), lax.rem(dp, 2)
    l, core = m // 2, lax.rem(m, 2)

    def device_at(x, z, h, m):
        return (x * 8 + z * 2 + h, m)

    pair = device_at(x, z, h, l * 2 + 1 - core)
    far = device_at(x, z, h, (1 - l) * 2 + core)
    along_x = [device_at(lax.rem(x + d, 4), z, h, m) for d in (1, 3)]
    along_z = [device_at(x, lax.rem(z + d, 4), h, m) for d in (1, 3)]
    across_h = device_at(x, z, 1 - h, m)

    acts_in = pltpu.make_async_copy(acts_hbm, r["acts"], r["in_sem"].at[0])
    acts_in.start()

    barrier = pltpu.get_barrier_semaphore()
    for other in (pair, far, *along_x, *along_z, across_h):
        pl.semaphore_signal(barrier, inc=1, device_id=other, device_id_type=MESH)

    def greet(sender, carry):
        @pl.when(jnp.logical_not(jnp.logical_and(sender == dp, m == x)))
        def _():
            pl.semaphore_signal(barrier, inc=1, device_id=(sender, x), device_id_type=MESH)
        return carry

    lax.fori_loop(0, 32, greet, 0)
    pl.semaphore_wait(barrier, jnp.where(m == x, 38, 39))

    def own(cc, g):
        return (true_ref, sampled_ref)[g].at[:, pl.ds(cc * BLOCK, BLOCK)]

    def lanes(g):
        return pl.ds(g * BLOCK, BLOCK)

    pieces = [(cc, g) for cc in range(2) for g in range(2)]
    inputs, pairs, fars, fwds, started = [], [], [], [], []
    for i, (cc, g) in enumerate(pieces):
        near_place = r["cots0"].at[core * 2 + cc, :, lanes(g)]
        far_place = r[f"cots{1 + cc}"].at[core, :, lanes(g)]
        fars.append(remote(own(cc, g), far_place, r["far_send"].at[i], r["far_recv"].at[i], far))
        pairs.append(remote(own(cc, g), near_place, r["pair_send"].at[i], r["pair_recv"].at[i], pair))
        inputs.append(pltpu.make_async_copy(own(cc, g), near_place, r["in_sem"].at[1 + i]))
    for copies in (fars, pairs, inputs):
        for copy in copies:
            copy.start()
    acts_in.wait()

    def transpose(row, carry):
        r["acts_t"][row] = r["acts"][:, pl.ds(pl.multiple_of(row * BLOCK, BLOCK), BLOCK)].T
        return carry

    lax.fori_loop(0, TILE_ROWS, transpose, 0)

    def products(w):
        group, first, n = WAVES[w]
        cots, part = r[f"cots{group}"], r[f"part{w}"]

        def one(i, carry):
            for u in range(2):
                s = 2 * i + u
                row = table_ref[ROWS_AT[group] + first + s]
                col = table_ref[COLS_AT[group] + first + s]
                tile = jnp.dot(r["acts_t"][row], cots[col], preferred_element_type=F32)
                for g in range(2):
                    part[g, :, s] = tile[:, g * BLOCK : (g + 1) * BLOCK].reshape(16, 8, BLOCK)
            return carry

        lax.fori_loop(0, n // 2, one, 0)

    def ring_open(send, recv, pos, neighbours, chunk, relay, final):
        up, down = neighbours
        nxt, opposite, prv = (lax.rem(pos + d, 4) for d in (1, 2, 3))
        copies = [
            remote(chunk(opposite, 0), relay.at[0], send.at[0], recv.at[0], up),
            remote(chunk(opposite, 1), relay.at[1], send.at[1], recv.at[1], down),
            remote(chunk(nxt, 1), final.at[0], send.at[2], recv.at[2], up),
            remote(chunk(prv, 0), final.at[1], send.at[3], recv.at[3], down),
            remote(relay.at[0], final.at[2], send.at[4], recv.at[4], up),
            remote(relay.at[1], final.at[3], send.at[5], recv.at[5], down),
        ]
        for copy in copies[:4]:
            copy.start()
        started.extend(copies)
        return copies

    def ring_turn(copies, pos, chunk, relay, add):
        for i, d in enumerate((1, 3)):
            copies[i].wait_recv()
            add(relay.at[i], (relay.at[i], chunk(lax.rem(pos + d, 4), i)))
            copies[4 + i].start()

    def ring_close(copies, pos, chunk, final, add, result):
        for copy in copies[2:]:
            copy.wait_recv()
        add(result(0), (chunk(pos, 0), final.at[1], final.at[2]))
        add(result(1), (chunk(pos, 1), final.at[0], final.at[3]))

    def add_big(dst, srcs):
        for i in range(2):
            total = srcs[0][i] + srcs[1][i]
            for src in srcs[2:]:
                total = total + src[i]
            dst[i] = total

    def add_small(dst, srcs):
        total = srcs[0][...] + srcs[1][...]
        for src in srcs[2:]:
            total = total + src[...]
        dst[...] = total

    streams = ((x, along_x, z, along_z), (z, along_z, x, along_x))
    first_ring, second_ring, swaps = {}, {}, {}

    def chunk1(w, s):
        return lambda p, half: r[f"part{w}"].at[s, pl.ds(p * 4 + half * 2, 2)]

    def chunk2(w, s):
        half_n = WAVES[w][2] // 2
        return lambda p, half: r[f"mid{w}"].at[s, p, pl.ds(half * half_n, half_n)]

    def open_first(w):
        for s, (pos, near, _, _) in enumerate(streams):
            first_ring[w, s] = ring_open(
                r[f"ring_send{w}"].at[s, 0], r[f"ring_recv{w}"].at[s, 0], pos, near, chunk1(w, s),
                r[f"relay1_{w}"].at[s], r[f"final1_{w}"].at[s],
            )

    def turn_first(w):
        for s, (pos, _, _, _) in enumerate(streams):
            ring_turn(first_ring[w, s], pos, chunk1(w, s), r[f"relay1_{w}"].at[s], add_big)

    def close_first(w):
        for s, (pos, _, pos2, near2) in enumerate(streams):
            ring_close(
                first_ring[w, s], pos, chunk1(w, s), r[f"final1_{w}"].at[s], add_big,
                lambda half: r[f"mid{w}"].at[s, pl.ds(half * 2, 2)],
            )
            second_ring[w, s] = ring_open(
                r[f"ring_send{w}"].at[s, 1], r[f"ring_recv{w}"].at[s, 1], pos2, near2, chunk2(w, s),
                r[f"relay2_{w}"].at[s], r[f"final2_{w}"].at[s],
            )

    def turn_second(w):
        for s, (_, _, pos2, _) in enumerate(streams):
            ring_turn(second_ring[w, s], pos2, chunk2(w, s), r[f"relay2_{w}"].at[s], add_small)

    def close_second(w):
        half_n = WAVES[w][2] // 2
        for s, (_, _, pos2, _) in enumerate(streams):
            ring_close(
                second_ring[w, s], pos2, chunk2(w, s), r[f"final2_{w}"].at[s], add_small,
                lambda half: r[f"last{w}"].at[s, pl.ds(half * half_n, half_n)],
            )
        swaps[w] = remote(
            r[f"last{w}"].at[1 - h], r[f"over{w}"], r[f"swap_send{w}"].at[0], r[f"swap_recv{w}"].at[0], across_h
        )
        swaps[w].start()
        started.append(swaps[w])

    def owner(g, t):
        return m * 8 + t // 2, (l if g == 0 else 1 - l) * 2 + lax.rem(t, 2)

    def itself(g, t):
        return jnp.logical_and(owner(g, t)[0] == dp, owner(g, t)[1] == m)

    def spot(g):
        return r["landed"].at[dp] if g == 0 else r["landed"].at[dp, g - 1]

    def outgoing(g, t):
        return remote(r[f"dense{g}"].at[t], spot(g), r[f"out_send{g}"].at[t], r[f"out_recv{g}"].at[dp], owner(g, t))

    def deliver(g):
        tiles, dense = r[f"tiles{g}"], r[f"dense{g}"]
        for w, (group, first, n) in enumerate(WAVES):
            if group == g:
                swaps[w].wait_recv()
                tiles[pl.ds(first, n)] = r[f"last{w}"][h] + r[f"over{w}"][...]
        tiles[GROUP_SLOTS[g]] = jnp.zeros((8, BLOCK), F32)

        def one(t, carry):
            core_to = lax.rem(t, 2)
            for lo in range(2):
                row = (t // 2) * 2 + lo
                if g == 0:
                    for cc in range(2):
                        dense[t, cc, lo] = tiles[table_ref[PLACES_AT[g] + row * 4 + core_to * 2 + cc]]
                else:
                    dense[t, lo] = tiles[table_ref[PLACES_AT[g] + row * 2 + core_to]]

            @pl.when(itself(g, t))
            def _():
                pltpu.make_async_copy(dense.at[t], spot(g), r[f"out_recv{g}"].at[dp]).start()

            @pl.when(jnp.logical_not(itself(g, t)))
            def _():
                outgoing(g, t).start()

            return carry

        lax.fori_loop(0, 16, one, 0)

    def drain(g):
        def one(t, carry):
            @pl.when(jnp.logical_not(itself(g, t)))
            def _():
                outgoing(g, t).wait_send()

            return carry

        lax.fori_loop(0, 16, one, 0)

    def forward(cc):
        for i, (piece_cc, g) in enumerate(pieces):
            if piece_cc == cc:
                fars[i].wait_recv()
                place = r[f"cots{1 + cc}"].at[core, :, lanes(g)]
                copy = remote(place, place, r["fwd_send"].at[i], r["fwd_recv"].at[i], pair)
                copy.start()
                fwds.append(copy)

    def forwarded(cc):
        for copy in fwds[cc * 2 : cc * 2 + 2]:
            copy.wait_recv()

    for copy in inputs:
        copy.wait()
    for copy in pairs:
        copy.wait_recv()
    products(0)
    open_first(0)
    products(1)
    open_first(1)
    turn_first(0)
    forward(0)
    turn_first(1)
    forwarded(0)
    products(2)
    open_first(2)
    close_first(0)
    close_first(1)
    turn_first(2)
    forward(1)
    forwarded(1)
    products(3)
    open_first(3)
    turn_second(0)
    turn_second(1)
    close_second(0)
    close_second(1)
    close_first(2)
    turn_first(3)
    turn_second(2)
    deliver(0)
    close_second(2)
    close_first(3)
    deliver(1)
    turn_second(3)
    close_second(3)
    deliver(2)

    def arrived(g):
        def one(i, carry):
            place = r["landed"].at[i] if g == 0 else r["landed"].at[i, g - 1]
            pltpu.make_async_copy(place, place, r[f"out_recv{g}"].at[i]).wait()
            return carry

        lax.fori_loop(0, 32, one, 0)

    @pl.when(m // 2 == x // 2)
    def _():
        arrived(0)

    @pl.when(m // 2 != x // 2)
    def _():
        arrived(1)
        arrived(2)

    def finish(strip, carry):
        from_true = strip * 2
        from_sampled = (lax.rem(strip, 4) * 4 + strip // 4) * 2 + 1
        for cc in range(2):
            for lo in range(2):
                at = (pl.ds(pl.multiple_of(lo * BLOCK + strip * 8, 8), 8), pl.ds(cc * BLOCK, BLOCK))
                out_ref[(0, *at)] = r["landed"][from_true, cc, lo]
                out_ref[(1, *at)] = r["landed"][from_sampled, cc, lo]
        return carry

    lax.fori_loop(0, 16, finish, 0)

    for copy in (*fars, *pairs, *fwds, *started):
        copy.wait_send()
    for g in range(3):
        drain(g)


def reduced_tiles(table, activations, cot_true, cot_sampled):
    vmem = pl.BlockSpec(memory_space=pltpu.VMEM)
    smem = pl.BlockSpec(memory_space=pltpu.SMEM)
    hbm = pl.BlockSpec(memory_space=pl.ANY)
    return pl.pallas_call(
        kernel,
        out_shape=jax.ShapeDtypeStruct((2, 2 * BLOCK, 2 * BLOCK), F32),
        in_specs=[smem, hbm, hbm, hbm],
        out_specs=vmem,
        scratch_shapes=list(scratch_list(activations.shape[0]).values()),
        compiler_params=pltpu.CompilerParams(
            collective_id=0, has_side_effects=True, vmem_limit_bytes=60 << 20
        ),
        name="reduced_tiles",
    )(table, activations, cot_true, cot_sampled)


def group_columns(half, group):
    if group == 0:
        return tuple(half * 4 + k for k in range(4))
    return tuple((1 - half) * 4 + k * 2 + group - 1 for k in range(2))


def tables(tile_mask, m, round_):
    own_rows = lax.dynamic_slice_in_dim(tile_mask, m * TILE_ROWS, TILE_ROWS, 0) > 0
    parts = []
    for group, n in enumerate(GROUP_SLOTS):
        first, second = (own_rows[:, jnp.array(group_columns(half, group))] for half in range(2))
        kept = jnp.where(m < 2, first, second).reshape(-1)
        cols = GROUP_COLS[group]
        index = jnp.arange(TILE_ROWS * cols)
        slot = jnp.sum(kept[None, :] & (index[None, :] < index[:, None]), axis=1) - round_ * n
        here = kept & (slot >= 0) & (slot < n)
        chosen = here[None, :] & (slot[None, :] == jnp.arange(n)[:, None])
        parts.append(jnp.sum(jnp.where(chosen, index[None, :] // cols, 0), axis=1))
        parts.append(jnp.sum(jnp.where(chosen, index[None, :] % cols, 0), axis=1))
        parts.append(jnp.where(here, slot, n))
    return jnp.concatenate(parts).astype(I32)


def rounds_of(tile_mask):
    counts = jnp.sum(tile_mask.reshape(4, TILE_ROWS, 8) > 0, axis=1)
    rounds = jnp.int32(1)
    for source in range(4):
        for group, n in enumerate(GROUP_SLOTS):
            filled = sum(counts[source, col] for col in group_columns(source // 2, group))
            rounds = jnp.maximum(rounds, (filled + n - 1) // n)
    return rounds


def on_device(activations, cot_true, cot_sampled, tile_mask, moment, curvature):
    m = lax.axis_index("mp")
    dp = lax.axis_index("dp")
    tokens_all = activations.shape[0] * lax.axis_size("dp")
    rounds = rounds_of(tile_mask)

    def step(state):
        round_, total = state
        table = tables(tile_mask, m, round_)
        return round_ + 1, total + reduced_tiles(table, activations, cot_true, cot_sampled)

    start = (jnp.int32(0), jnp.zeros((2, 2 * BLOCK, 2 * BLOCK), jnp.float32))
    _, sums = lax.while_loop(lambda state: state[0] < rounds, step, start)
    owned = lax.dynamic_slice(tile_mask, (dp * 2, m * 2), (2, 2))
    owned_mask = jnp.repeat(jnp.repeat(owned, BLOCK, axis=0), BLOCK, axis=1).astype(jnp.float32)
    grads = sums * (1.0 / tokens_all)
    moment_new = BETA_ONE * moment + (1.0 - BETA_ONE) * grads[0]
    hessian = tokens_all * grads[1] * grads[1]
    curvature_next = BETA_TWO * curvature + (1.0 - BETA_TWO) * hessian
    update = jnp.clip(moment_new / (GAMMA_CLIP * curvature_next), -1.0, 1.0) * owned_mask
    return (update, curvature_next * owned_mask)


def solution(mesh):
    return jax.shard_map(
        on_device,
        mesh=mesh,
        in_specs=(P("dp", "mp"), P("dp", "mp"), P("dp", "mp"), P(), P("dp", "mp"), P("dp", "mp")),
        out_specs=(P("dp", "mp"), P("dp", "mp")),
        check_vma=False,
    )
```

time: 554 us -> 121 us (0.22)
  waiting for transfers between devices: 516 us -> 0 us
  Pallas kernels: 0 us -> 84.1 us
  matrix products: 16.2 us -> 0 us
  between operations: 14.1 us -> 21 us
    reduce_scatter x1 -> x0, waiting for transfers between devices: 361 us -> none  [on_device(): lax.psum_scatter(product * inv_tokens * jnp.concatenate([row_mask, row_ma...]
    all_gather x1 -> x0, waiting for transfers between devices: 155 us -> none  [on_device(): panel = lax.all_gather(activations, 'mp', axis=1, tiled=True)]
    pallas_call x0 -> x1, Pallas kernels: none -> 84.1 us  [reduced_tiles(): pl.pallas_call(kernel, out_shape=jax.ShapeDtypeStruct((2, 2 * BLOCK, 2 *...]
    dot_general x1 -> x0, matrix products: 16.2 us -> none  [on_device(): lax.dot_general(panel, cotangents, CONTRACT, preferred_element_type=jnp.f...]
  transfers between devices with their start and end apart: 2 -> 0, of which waited for: 2 -> 0; matrix products, arithmetic and copies ran while one was open for 0% -> 0% of each run, Pallas kernels for 0% -> 0%
where the time goes in v2:
time: 121 us; the launch traced here: 120 us
  Pallas kernels  84.1 us (70%)
  between operations  21 us (17%)
  other arithmetic  7.89 us (7%)
  local copies, waits for them, and re-layouts  6.88 us (6%)
    pallas_call x1, Pallas kernels, reduced_tiles(): pl.pallas_call(kernel, out_shape=jax.ShapeDtypeStruct((2, 2 * BLOCK, 2 *...  84.1 us
    gather x6, local copies, waits for them, and re-layouts, tables(): own_rows[:, jnp.array(group_columns(half, group))]  3.37 us
    gather x6, other arithmetic, tables(): own_rows[:, jnp.array(group_columns(half, group))]  2.66 us

profile of v2, /device:TPU:5, one launch (start us, length us, event | category | flops | bytes accessed | tf_op | source)
XLA Modules:
  0.0 120.0 jit_solution(18350750772397718743)
XLA Ops:
  0.6 0.7 compare_convert_fusion
  1.4 0.2 reduce_sum.135
  1.6 0.7 fusion.12
  8.7 0.7 fusion.13
  23.3 0.8 dynamic-slice_compare_fusion
  24.1 0.6 gather_fusion
  24.7 0.1 copy.35
  24.8 0.6 gather_fusion.3
  25.3 0.1 copy.38
  25.4 0.7 pad_clamp_fusion.4
  26.1 0.6 gather_fusion.1
  26.7 0.1 copy.36
  26.8 0.7 pad_clamp_fusion.3
  27.4 0.6 gather_fusion.2
  28.0 0.1 copy.37
  28.1 0.7 pad_clamp_fusion.1
  28.7 0.6 gather_fusion.4
  29.3 0.1 copy.39
  29.4 0.7 pad_clamp_fusion
  30.1 0.6 gather_fusion.5
  30.8 87.0 %while.14 = (s32[]{:T(128)}, f32[2,256,256]{2,1,0:T(8,128)S(1)}, s32[]{:T(128)}, pred[]{:T(512)}, pred[16,4]{1,0:T(8,128)(4,1)S(1)}, /*index=5*/pred[16,4]{1,0:T...) while((s32[]{:T(128)}, f32[2,256,256]{2,1,0:T(8,128)S(1)}, ...), condition=%wide.region_11.12_spmd, body=%wide.region_1.11_spmd.sunk | while | flops 174096 | bytes 1581355 | solution.py:438
  30.9 0.1 convert_reduce_fusion.7
  31.2 0.1 convert_reduce_fusion.8
  31.3 0.1 select_reduce_fusion.9
  31.6 0.1 convert_reduce_fusion.6
  31.7 0.1 select_reduce_fusion.8
  31.9 0.7 concatenate.4.refs_0_
  32.5 84.1 %reduced_tiles.6 = f32[2,256,256]{2,1,0:T(8,128)} custom-call(s32[244]{0:T(256)} %concatenate.4.refs_0_, bf16[1024,2048]{1,0:T(8,128)(2,1)} %get-tuple-element.650.refs_1_, bf16[1024,256]{1,0:T(8,128)(2,1)} %get-tuple-element.651.refs_2_, bf16[1024,256]{1,0:T(8,128)(2,1)} %get-tuple-element.652.refs_3_), custom_call_target="tpu_custom_call" | custom-call | tf_op jit(solution)/shard_map/while/body/reduced_tiles/pallas_call | solution.py:380
  116.6 1.2 add.372
  117.8 0.8 dynamic-slice_convert_fusion
  118.7 0.3 broadcast_in_dim.125
  119.1 0.9 bitcast_multiply_fusion
  (27 shorter events, 0.8 us)
Async XLA Ops:
  30.8 88.3 %copy-start = (f32[256,256]{1,0:T(8,128)S(1)}, f32[256,256]{1,0:T(8,128)}, u32[]{:S(2)}) copy-start(f32[256,256]{1,0:T(8,128)} %param.19) | copy-start | bytes 786436
  30.8 88.3 %copy-start.1 = (f32[256,256]{1,0:T(8,128)S(1)}, f32[256,256]{1,0:T(8,128)}, u32[]{:S(2)}) copy-start(f32[256,256]{1,0:T(8,128)} %param.18) | copy-start | bytes 786436

commit v3 on v2

--- a/solution.py
+++ b/solution.py
@@ -1,3 +1,5 @@
+import functools
+
 import jax
 import jax.numpy as jnp
 from jax import lax
@@ -18,13 +20,10 @@
 GROUP_SLOTS = tuple(sum(n for g, _, n in WAVES if g == group) for group in range(3))
 TILE_ROWS = 16
 
-ROWS_AT, COLS_AT, PLACES_AT = [], [], []
-TABLE_SIZE = 0
-for _slots, _cols in zip(GROUP_SLOTS, GROUP_COLS):
-    ROWS_AT.append(TABLE_SIZE)
-    COLS_AT.append(TABLE_SIZE + _slots)
-    PLACES_AT.append(TABLE_SIZE + 2 * _slots)
-    TABLE_SIZE += 2 * _slots + TILE_ROWS * _cols
+FIRST_COL = (0, 4, 6)
+LIST_AT = TILE_ROWS
+ROUNDS_AT = TILE_ROWS + 6
+TABLE = (TILE_ROWS + 8, BLOCK)
 
 
 def remote(src, dst, send_sem, recv_sem, device):
@@ -37,6 +36,8 @@
 def scratch_list(tokens):
     dma = pltpu.SemaphoreType.DMA
     shapes = dict(
+        moment=pltpu.VMEM((2 * BLOCK, 2 * BLOCK), F32),
+        curvature=pltpu.VMEM((2 * BLOCK, 2 * BLOCK), F32),
         acts=pltpu.VMEM((tokens, TILE_ROWS * BLOCK), BF16),
         acts_t=pltpu.VMEM((TILE_ROWS, BLOCK, tokens), BF16),
         landed=pltpu.VMEM((32, 2, 2, 8, BLOCK), F32),
@@ -70,11 +71,12 @@
     return shapes
 
 
-def kernel(*refs):
+def kernel(tokens_all, *refs):
     refs = list(refs)
     names = list(scratch_list(8))
     r = dict(zip(names, refs[-len(names):]))
-    table_ref, acts_hbm, true_ref, sampled_ref, out_ref = refs[: -len(names)]
+    table_ref, mask_ref, acts_hbm, true_ref, sampled_ref, moment_hbm, curvature_hbm, sums_in = refs[:8]
+    update_ref, new_curvature_ref, sums_ref = refs[8 : -len(names)]
 
     dp = lax.axis_index("dp")
     m = lax.axis_index("mp")
@@ -123,6 +125,10 @@
     for copies in (fars, pairs, inputs):
         for copy in copies:
             copy.start()
+    moment_in = pltpu.make_async_copy(moment_hbm, r["moment"], r["in_sem"].at[5])
+    curvature_in = pltpu.make_async_copy(curvature_hbm, r["curvature"], r["in_sem"].at[6])
+    moment_in.start()
+    curvature_in.start()
     acts_in.wait()
 
     def transpose(row, carry):
@@ -138,8 +144,8 @@
         def one(i, carry):
             for u in range(2):
                 s = 2 * i + u
-                row = table_ref[ROWS_AT[group] + first + s]
-                col = table_ref[COLS_AT[group] + first + s]
+                row = table_ref[LIST_AT + 2 * group, first + s]
+                col = table_ref[LIST_AT + 2 * group + 1, first + s]
                 tile = jnp.dot(r["acts_t"][row], cots[col], preferred_element_type=F32)
                 for g in range(2):
                     part[g, :, s] = tile[:, g * BLOCK : (g + 1) * BLOCK].reshape(16, 8, BLOCK)
@@ -263,9 +269,9 @@
                 row = (t // 2) * 2 + lo
                 if g == 0:
                     for cc in range(2):
-                        dense[t, cc, lo] = tiles[table_ref[PLACES_AT[g] + row * 4 + core_to * 2 + cc]]
+                        dense[t, cc, lo] = tiles[table_ref[row, core_to * 2 + cc]]
                 else:
-                    dense[t, lo] = tiles[table_ref[PLACES_AT[g] + row * 2 + core_to]]
+                    dense[t, lo] = tiles[table_ref[row, FIRST_COL[g] + core_to]]
 
             @pl.when(itself(g, t))
             def _():
@@ -346,6 +352,9 @@
 
         lax.fori_loop(0, 32, one, 0)
 
+    moment_in.wait()
+    curvature_in.wait()
+
     @pl.when(m // 2 == x // 2)
     def _():
         arrived(0)
@@ -361,8 +370,19 @@
         for cc in range(2):
             for lo in range(2):
                 at = (pl.ds(pl.multiple_of(lo * BLOCK + strip * 8, 8), 8), pl.ds(cc * BLOCK, BLOCK))
-                out_ref[(0, *at)] = r["landed"][from_true, cc, lo]
-                out_ref[(1, *at)] = r["landed"][from_sampled, cc, lo]
+                sum_true = r["landed"][from_true, cc, lo] + sums_in[(0, *at)]
+                sum_sampled = r["landed"][from_sampled, cc, lo] + sums_in[(1, *at)]
+                sums_ref[(0, *at)] = sum_true
+                sums_ref[(1, *at)] = sum_sampled
+                grad_true = sum_true * (1.0 / tokens_all)
+                grad_sampled = sum_sampled * (1.0 / tokens_all)
+                moment_new = BETA_ONE * r["moment"][at] + (1.0 - BETA_ONE) * grad_true
+                hessian = tokens_all * grad_sampled * grad_sampled
+                curvature_next = BETA_TWO * r["curvature"][at] + (1.0 - BETA_TWO) * hessian
+                update = jnp.clip(moment_new / (GAMMA_CLIP * curvature_next), -1.0, 1.0)
+                kept = mask_ref[dp * 2 + lo, m * 2 + cc].astype(F32)
+                update_ref[at] = update * kept
+                new_curvature_ref[at] = curvature_next * kept
         return carry
 
     lax.fori_loop(0, 16, finish, 0)
@@ -373,77 +393,113 @@
         drain(g)
 
 
-def reduced_tiles(table, activations, cot_true, cot_sampled):
+def round_step(tokens_all, *args):
     vmem = pl.BlockSpec(memory_space=pltpu.VMEM)
     smem = pl.BlockSpec(memory_space=pltpu.SMEM)
     hbm = pl.BlockSpec(memory_space=pl.ANY)
+    block = jax.ShapeDtypeStruct((2 * BLOCK, 2 * BLOCK), F32)
     return pl.pallas_call(
-        kernel,
-        out_shape=jax.ShapeDtypeStruct((2, 2 * BLOCK, 2 * BLOCK), F32),
-        in_specs=[smem, hbm, hbm, hbm],
-        out_specs=vmem,
-        scratch_shapes=list(scratch_list(activations.shape[0]).values()),
+        functools.partial(kernel, tokens_all),
+        out_shape=(block, block, jax.ShapeDtypeStruct((2, 2 * BLOCK, 2 * BLOCK), F32)),
+        in_specs=[smem, smem, hbm, hbm, hbm, hbm, hbm, vmem],
+        out_specs=(vmem,) * 3,
+        scratch_shapes=list(scratch_list(args[2].shape[0]).values()),
         compiler_params=pltpu.CompilerParams(
             collective_id=0, has_side_effects=True, vmem_limit_bytes=60 << 20
         ),
-        name="reduced_tiles",
-    )(table, activations, cot_true, cot_sampled)
-
-
-def group_columns(half, group):
-    if group == 0:
-        return tuple(half * 4 + k for k in range(4))
-    return tuple((1 - half) * 4 + k * 2 + group - 1 for k in range(2))
-
-
-def tables(tile_mask, m, round_):
-    own_rows = lax.dynamic_slice_in_dim(tile_mask, m * TILE_ROWS, TILE_ROWS, 0) > 0
-    parts = []
-    for group, n in enumerate(GROUP_SLOTS):
-        first, second = (own_rows[:, jnp.array(group_columns(half, group))] for half in range(2))
-        kept = jnp.where(m < 2, first, second).reshape(-1)
-        cols = GROUP_COLS[group]
-        index = jnp.arange(TILE_ROWS * cols)
-        slot = jnp.sum(kept[None, :] & (index[None, :] < index[:, None]), axis=1) - round_ * n
-        here = kept & (slot >= 0) & (slot < n)
-        chosen = here[None, :] & (slot[None, :] == jnp.arange(n)[:, None])
-        parts.append(jnp.sum(jnp.where(chosen, index[None, :] // cols, 0), axis=1))
-        parts.append(jnp.sum(jnp.where(chosen, index[None, :] % cols, 0), axis=1))
-        parts.append(jnp.where(here, slot, n))
-    return jnp.concatenate(parts).astype(I32)
-
-
-def rounds_of(tile_mask):
-    counts = jnp.sum(tile_mask.reshape(4, TILE_ROWS, 8) > 0, axis=1)
-    rounds = jnp.int32(1)
-    for source in range(4):
-        for group, n in enumerate(GROUP_SLOTS):
-            filled = sum(counts[source, col] for col in group_columns(source // 2, group))
-            rounds = jnp.maximum(rounds, (filled + n - 1) // n)
-    return rounds
+        name="round_step",
+    )(*args)
+
+
+def table_kernel(round_ref, mask_ref, table_ref):
+    m = lax.axis_index("mp")
+    half = m // 2
+    own = mask_ref[pl.ds(pl.multiple_of(m * TILE_ROWS, TILE_ROWS), TILE_ROWS), :]
+    kept_all = jnp.where(own > 0, 1, 0)
+    row_index = lax.broadcasted_iota(I32, (TILE_ROWS, 1), 0)
+    slot_index = lax.broadcasted_iota(I32, (TILE_ROWS, BLOCK), 1)
+    lane = lax.broadcasted_iota(I32, (TILE_ROWS, BLOCK), 1)
+    before_rows = lax.broadcasted_iota(I32, (TILE_ROWS, TILE_ROWS), 1) < lax.broadcasted_iota(
+        I32, (TILE_ROWS, TILE_ROWS), 0
+    )
+    place = jnp.zeros((TILE_ROWS, BLOCK), I32)
+    lines = []
+    for g, cols in enumerate(GROUP_COLS):
+        n = GROUP_SLOTS[g]
+        near, other = (
+            [half_ * 4 + k for k in range(4)] if g == 0 else [(1 - half_) * 4 + k * 2 + g - 1 for k in range(2)]
+            for half_ in range(2)
+        )
+        kept = [
+            jnp.where(half == 0, kept_all[:, near[k] : near[k] + 1], kept_all[:, other[k] : other[k] + 1])
+            for k in range(cols)
+        ]
+        per_row = functools.reduce(lambda p, q: p + q, kept)
+        turned = jnp.sum(
+            jnp.where(
+                lax.broadcasted_iota(I32, (TILE_ROWS, TILE_ROWS), 0)
+                == lax.broadcasted_iota(I32, (TILE_ROWS, TILE_ROWS), 1),
+                per_row, 0,
+            ),
+            axis=0, keepdims=True,
+        )
+        seen = jnp.sum(jnp.where(before_rows, turned, 0), axis=1, keepdims=True) - round_ref[0] * n
+        rows_line = jnp.zeros((1, BLOCK), I32)
+        cols_line = jnp.zeros((1, BLOCK), I32)
+        for k in range(cols):
+            here = (kept[k] > 0) & (seen >= 0) & (seen < n)
+            place = jnp.where(lane == FIRST_COL[g] + k, jnp.where(here, seen, n), place)
+            chosen = jnp.where(here, seen, -1) == slot_index
+            rows_line = rows_line + jnp.sum(jnp.where(chosen, row_index, 0), axis=0, keepdims=True)
+            cols_line = cols_line + jnp.sum(jnp.where(chosen, k, 0), axis=0, keepdims=True)
+            seen = seen + kept[k]
+        lines += [rows_line, cols_line]
+
+    counts = jnp.sum(jnp.where(mask_ref[...] > 0, 1, 0).reshape(4, TILE_ROWS, 8), axis=1)
+    source = lax.broadcasted_iota(I32, (4, 8), 0)
+    column = lax.broadcasted_iota(I32, (4, 8), 1)
+    near = (source // 2) == (column // 4)
+    even = lax.rem(column, 2) == 0
+    needed = jnp.zeros((4, 1), I32)
+    for g, inside in enumerate((near, ~near & even, ~near & ~even)):
+        filled = jnp.sum(jnp.where(inside, counts, 0), axis=1, keepdims=True)
+        rounds = sum(jnp.where(filled > n * GROUP_SLOTS[g], 1, 0) for n in range(TILE_ROWS * GROUP_COLS[g] // GROUP_SLOTS[g] + 1))
+        needed = jnp.maximum(needed, rounds)
+    lines.append(jnp.broadcast_to(jnp.max(needed, axis=0, keepdims=True), (1, BLOCK)))
+    table_ref[pl.ds(0, TILE_ROWS)] = place
+    for i, line in enumerate(lines):
+        table_ref[pl.ds(TILE_ROWS + i, 1)] = line
+    table_ref[pl.ds(TILE_ROWS + len(lines), 1)] = jnp.zeros((1, BLOCK), I32)
+
+
+def table_of(tile_mask, round_):
+    return pl.pallas_call(
+        table_kernel,
+        out_shape=jax.ShapeDtypeStruct(TABLE, I32),
+        in_specs=[pl.BlockSpec(memory_space=pltpu.SMEM), pl.BlockSpec(memory_space=pltpu.VMEM)],
+        out_specs=pl.BlockSpec(memory_space=pltpu.VMEM),
+        name="tables",
+    )(round_.reshape(1), tile_mask)
 
 
 def on_device(activations, cot_true, cot_sampled, tile_mask, moment, curvature):
-    m = lax.axis_index("mp")
-    dp = lax.axis_index("dp")
     tokens_all = activations.shape[0] * lax.axis_size("dp")
-    rounds = rounds_of(tile_mask)
+
+    def more(state):
+        round_, rounds = state[:2]
+        return round_ < rounds
 
     def step(state):
-        round_, total = state
-        table = tables(tile_mask, m, round_)
-        return round_ + 1, total + reduced_tiles(table, activations, cot_true, cot_sampled)
-
-    start = (jnp.int32(0), jnp.zeros((2, 2 * BLOCK, 2 * BLOCK), jnp.float32))
-    _, sums = lax.while_loop(lambda state: state[0] < rounds, step, start)
-    owned = lax.dynamic_slice(tile_mask, (dp * 2, m * 2), (2, 2))
-    owned_mask = jnp.repeat(jnp.repeat(owned, BLOCK, axis=0), BLOCK, axis=1).astype(jnp.float32)
-    grads = sums * (1.0 / tokens_all)
-    moment_new = BETA_ONE * moment + (1.0 - BETA_ONE) * grads[0]
-    hessian = tokens_all * grads[1] * grads[1]
-    curvature_next = BETA_TWO * curvature + (1.0 - BETA_TWO) * hessian
-    update = jnp.clip(moment_new / (GAMMA_CLIP * curvature_next), -1.0, 1.0) * owned_mask
-    return (update, curvature_next * owned_mask)
+        round_, _, _, _, sums = state
+        table = table_of(tile_mask, round_)
+        update, new_curvature, sums = round_step(
+            tokens_all, table, tile_mask, activations, cot_true, cot_sampled, moment, curvature, sums
+        )
+        return round_ + 1, table[ROUNDS_AT, 0], update, new_curvature, sums
+
+    start = (jnp.int32(0), jnp.int32(1), moment, curvature, jnp.zeros((2, 2 * BLOCK, 2 * BLOCK), F32))
+    _, _, update, new_curvature, _ = lax.while_loop(more, step, start)
+    return update, new_curvature
 
 
 def solution(mesh):

time: 121 us -> 97.2 us (0.80)
  between operations: 21 us -> 0.64 us
  other arithmetic: 7.89 us -> 0 us
  local copies, waits for them, and re-layouts: 6.88 us -> 9.47 us
  Pallas kernels: 84.1 us -> 86.1 us
    unnamed x4, local copies, waits for them, and re-layouts: 0.01 us -> 6.66 us
    gather x6 -> x0, local copies, waits for them, and re-layouts: 3.37 us -> none  [tables(): own_rows[:, jnp.array(group_columns(half, group))]]
    gather x6 -> x0, other arithmetic: 2.66 us -> none  [tables(): own_rows[:, jnp.array(group_columns(half, group))]]
    pallas_call x1 -> x2, Pallas kernels: 84.1 us -> 86.1 us  [the longest x1 85 us: round_step(): pl.pallas_call(functools.partial(kernel, tokens_all), out_shape=(block, b...]
    convert_element_type x2 -> x0, other arithmetic: 1.46 us -> none  [the longest x1 0.77 us: on_device(): jnp.repeat(jnp.repeat(owned, BLOCK, axis=0), BLOCK, axis=1)]
where the time goes in v3:
time: 97.2 us; the launch traced here: 96.9 us
  Pallas kernels  86.1 us (89%)
  local copies, waits for them, and re-layouts  9.47 us (10%)
    pallas_call x1, Pallas kernels, round_step(): pl.pallas_call(functools.partial(kernel, tokens_all), out_shape=(block, b...  85 us
    unnamed x4, local copies, waits for them, and re-layouts  6.66 us

profile of v3, /device:TPU:5, one launch (start us, length us, event | category | flops | bytes accessed | tf_op | source)
XLA Modules:
  0.0 96.9 jit_solution(1980396282928948101)
XLA Ops:
  0.6 0.8 copy.8
  1.4 1.7 %copy.11 = f32[256,256]{1,0:T(8,128)} copy(f32[256,256]{1,0:T(8,128)} %param.12) | data formatting | bytes 524288
  3.1 1.7 %copy.12 = f32[256,256]{1,0:T(8,128)} copy(f32[256,256]{1,0:T(8,128)} %param.13) | data formatting | bytes 524288
  4.8 88.7 %while.16 = (s32[]{:T(128)}, s32[]{:T(128)}, f32[256,256]{1,0:T(8,128)}, f32[256,256]{1,0:T(8,128)}, f32[2,256,256]{2,1,0:T(8,128)S(1)}, /*index=5*/s32[64,8]{1,...) while((s32[]{:T(128)}, s32[]{:T(128)}, ...), condition=%wide.region_1.0_spmd, body=%wide.region_0.0_spmd.sunk | while | flops 2 | bytes 1048709 | solution.py:501
  4.8 0.8 copy.29.refs_7_
  5.6 1.1 %tables.1.refs_0_ = s32[24,128]{1,0:T(8,128)} custom-call(s32[1]{0:T(128)} %bitcast.4.round_ref, s32[64,8]{1,0:T(8,128)S(1)} %get-tuple-element.193.mask_ref.refs_1_), custom_call_target="tpu_custom_call" | custom-call | tf_op jit(solution)/shard_map/while/body/tables/pallas_call | solution.py:476
  6.7 1.2 %slice.5 = s32[1,1]{1,0:T(1,128)} slice(s32[24,128]{1,0:T(8,128)} %tables.1.refs_0_), slice={[22:23], [0:1]} | slice | bytes 8 | tf_op jit(solution)/shard_map/while/body/slice | solution.py:498
  7.9 85.0 %round_step.1 = (f32[256,256]{1,0:T(8,128)}, f32[256,256]{1,0:T(8,128)}, f32[2,256,256]{2,1,0:T(8,128)S(1)}) custom-call(s32[24,128]{1,0:T(8,128)} %tables.1.refs_0_, s32[64,8]{1,0:T(8,128)S(1)} %get-tuple-element.193.mask_ref.refs_1_, bf16[1024,2048]{1,0:T(8,128)(2,1)} %get-tuple-element.194.refs_2_, bf16[1024,256]{1,0:T(8,128)(2,1)} %get-tuple-element.195.refs_3_, ...), custom_call_target="tpu_custom_call" | custom-call | tf_op jit(solution)/shard_map/while/body/round_step/pallas_call | solution.py:401
  93.5 1.7 %copy.30 = f32[256,256]{1,0:T(8,128)} copy(f32[256,256]{1,0:T(8,128)} %get-tuple-element.202) | data formatting | bytes 524288
  95.2 1.7 %copy.31 = f32[256,256]{1,0:T(8,128)} copy(f32[256,256]{1,0:T(8,128)} %get-tuple-element.203) | data formatting | bytes 524288
  (1 shorter events, 0.0 us)

commit v4 on v3

--- a/solution.py
+++ b/solution.py
@@ -22,7 +22,6 @@
 
 FIRST_COL = (0, 4, 6)
 LIST_AT = TILE_ROWS
-ROUNDS_AT = TILE_ROWS + 6
 TABLE = (TILE_ROWS + 8, BLOCK)
 
 
@@ -36,12 +35,10 @@
 def scratch_list(tokens):
     dma = pltpu.SemaphoreType.DMA
     shapes = dict(
-        moment=pltpu.VMEM((2 * BLOCK, 2 * BLOCK), F32),
-        curvature=pltpu.VMEM((2 * BLOCK, 2 * BLOCK), F32),
         acts=pltpu.VMEM((tokens, TILE_ROWS * BLOCK), BF16),
         acts_t=pltpu.VMEM((TILE_ROWS, BLOCK, tokens), BF16),
         landed=pltpu.VMEM((32, 2, 2, 8, BLOCK), F32),
-        in_sem=dma((7,)),
+        in_sem=dma((5,)),
         pair_send=dma((4,)), pair_recv=dma((4,)),
         far_send=dma((4,)), far_recv=dma((4,)),
         fwd_send=dma((4,)), fwd_recv=dma((4,)),
@@ -71,12 +68,11 @@
     return shapes
 
 
-def kernel(tokens_all, *refs):
+def kernel(*refs):
     refs = list(refs)
     names = list(scratch_list(8))
     r = dict(zip(names, refs[-len(names):]))
-    table_ref, mask_ref, acts_hbm, true_ref, sampled_ref, moment_hbm, curvature_hbm, sums_in = refs[:8]
-    update_ref, new_curvature_ref, sums_ref = refs[8 : -len(names)]
+    table_ref, acts_hbm, true_ref, sampled_ref, sums_ref = refs[: -len(names)]
 
     dp = lax.axis_index("dp")
     m = lax.axis_index("mp")
@@ -125,10 +121,6 @@
     for copies in (fars, pairs, inputs):
         for copy in copies:
             copy.start()
-    moment_in = pltpu.make_async_copy(moment_hbm, r["moment"], r["in_sem"].at[5])
-    curvature_in = pltpu.make_async_copy(curvature_hbm, r["curvature"], r["in_sem"].at[6])
-    moment_in.start()
-    curvature_in.start()
     acts_in.wait()
 
     def transpose(row, carry):
@@ -352,9 +344,6 @@
 
         lax.fori_loop(0, 32, one, 0)
 
-    moment_in.wait()
-    curvature_in.wait()
-
     @pl.when(m // 2 == x // 2)
     def _():
         arrived(0)
@@ -370,19 +359,8 @@
         for cc in range(2):
             for lo in range(2):
                 at = (pl.ds(pl.multiple_of(lo * BLOCK + strip * 8, 8), 8), pl.ds(cc * BLOCK, BLOCK))
-                sum_true = r["landed"][from_true, cc, lo] + sums_in[(0, *at)]
-                sum_sampled = r["landed"][from_sampled, cc, lo] + sums_in[(1, *at)]
-                sums_ref[(0, *at)] = sum_true
-                sums_ref[(1, *at)] = sum_sampled
-                grad_true = sum_true * (1.0 / tokens_all)
-                grad_sampled = sum_sampled * (1.0 / tokens_all)
-                moment_new = BETA_ONE * r["moment"][at] + (1.0 - BETA_ONE) * grad_true
-                hessian = tokens_all * grad_sampled * grad_sampled
-                curvature_next = BETA_TWO * r["curvature"][at] + (1.0 - BETA_TWO) * hessian
-                update = jnp.clip(moment_new / (GAMMA_CLIP * curvature_next), -1.0, 1.0)
-                kept = mask_ref[dp * 2 + lo, m * 2 + cc].astype(F32)
-                update_ref[at] = update * kept
-                new_curvature_ref[at] = curvature_next * kept
+                sums_ref[(0, *at)] = r["landed"][from_true, cc, lo]
+                sums_ref[(1, *at)] = r["landed"][from_sampled, cc, lo]
         return carry
 
     lax.fori_loop(0, 16, finish, 0)
@@ -393,17 +371,15 @@
         drain(g)
 
 
-def round_step(tokens_all, *args):
-    vmem = pl.BlockSpec(memory_space=pltpu.VMEM)
+def round_step(*args):
     smem = pl.BlockSpec(memory_space=pltpu.SMEM)
     hbm = pl.BlockSpec(memory_space=pl.ANY)
-    block = jax.ShapeDtypeStruct((2 * BLOCK, 2 * BLOCK), F32)
     return pl.pallas_call(
-        functools.partial(kernel, tokens_all),
-        out_shape=(block, block, jax.ShapeDtypeStruct((2, 2 * BLOCK, 2 * BLOCK), F32)),
-        in_specs=[smem, smem, hbm, hbm, hbm, hbm, hbm, vmem],
-        out_specs=(vmem,) * 3,
-        scratch_shapes=list(scratch_list(args[2].shape[0]).values()),
+        kernel,
+        out_shape=jax.ShapeDtypeStruct((2, 2 * BLOCK, 2 * BLOCK), F32),
+        in_specs=[smem, hbm, hbm, hbm],
+        out_specs=pl.BlockSpec(memory_space=pltpu.VMEM),
+        scratch_shapes=list(scratch_list(args[1].shape[0]).values()),
         compiler_params=pltpu.CompilerParams(
             collective_id=0, has_side_effects=True, vmem_limit_bytes=60 << 20
         ),
@@ -411,7 +387,7 @@
     )(*args)
 
 
-def table_kernel(round_ref, mask_ref, table_ref):
+def table_kernel(round_ref, mask_ref, table_ref, rounds_ref):
     m = lax.axis_index("mp")
     half = m // 2
     own = mask_ref[pl.ds(pl.multiple_of(m * TILE_ROWS, TILE_ROWS), TILE_ROWS), :]
@@ -465,41 +441,45 @@
         filled = jnp.sum(jnp.where(inside, counts, 0), axis=1, keepdims=True)
         rounds = sum(jnp.where(filled > n * GROUP_SLOTS[g], 1, 0) for n in range(TILE_ROWS * GROUP_COLS[g] // GROUP_SLOTS[g] + 1))
         needed = jnp.maximum(needed, rounds)
-    lines.append(jnp.broadcast_to(jnp.max(needed, axis=0, keepdims=True), (1, BLOCK)))
+    rounds_ref[0] = jnp.max(needed)
+    lines.append(jnp.zeros((2, BLOCK), I32))
     table_ref[pl.ds(0, TILE_ROWS)] = place
-    for i, line in enumerate(lines):
-        table_ref[pl.ds(TILE_ROWS + i, 1)] = line
-    table_ref[pl.ds(TILE_ROWS + len(lines), 1)] = jnp.zeros((1, BLOCK), I32)
+    table_ref[pl.ds(TILE_ROWS, 8)] = jnp.concatenate(lines, axis=0)
 
 
 def table_of(tile_mask, round_):
     return pl.pallas_call(
         table_kernel,
-        out_shape=jax.ShapeDtypeStruct(TABLE, I32),
+        out_shape=(jax.ShapeDtypeStruct(TABLE, I32), jax.ShapeDtypeStruct((1,), I32)),
         in_specs=[pl.BlockSpec(memory_space=pltpu.SMEM), pl.BlockSpec(memory_space=pltpu.VMEM)],
-        out_specs=pl.BlockSpec(memory_space=pltpu.VMEM),
+        out_specs=(pl.BlockSpec(memory_space=pltpu.VMEM), pl.BlockSpec(memory_space=pltpu.SMEM)),
         name="tables",
     )(round_.reshape(1), tile_mask)
 
 
 def on_device(activations, cot_true, cot_sampled, tile_mask, moment, curvature):
+    m = lax.axis_index("mp")
+    dp = lax.axis_index("dp")
     tokens_all = activations.shape[0] * lax.axis_size("dp")
 
-    def more(state):
-        round_, rounds = state[:2]
-        return round_ < rounds
-
-    def step(state):
-        round_, _, _, _, sums = state
-        table = table_of(tile_mask, round_)
-        update, new_curvature, sums = round_step(
-            tokens_all, table, tile_mask, activations, cot_true, cot_sampled, moment, curvature, sums
-        )
-        return round_ + 1, table[ROUNDS_AT, 0], update, new_curvature, sums
-
-    start = (jnp.int32(0), jnp.int32(1), moment, curvature, jnp.zeros((2, 2 * BLOCK, 2 * BLOCK), F32))
-    _, _, update, new_curvature, _ = lax.while_loop(more, step, start)
-    return update, new_curvature
+    def one_round(round_):
+        table, rounds = table_of(tile_mask, round_)
+        return round_step(table, activations, cot_true, cot_sampled), rounds
+
+    sums, rounds = one_round(jnp.int32(0))
+    _, sums = lax.while_loop(
+        lambda state: state[0] < rounds[0],
+        lambda state: (state[0] + 1, state[1] + one_round(state[0])[0]),
+        (jnp.int32(1), sums),
+    )
+    owned = lax.dynamic_slice(tile_mask, (dp * 2, m * 2), (2, 2))
+    owned_mask = jnp.repeat(jnp.repeat(owned, BLOCK, axis=0), BLOCK, axis=1).astype(F32)
+    grads = sums * (1.0 / tokens_all)
+    moment_new = BETA_ONE * moment + (1.0 - BETA_ONE) * grads[0]
+    hessian = tokens_all * grads[1] * grads[1]
+    curvature_next = BETA_TWO * curvature + (1.0 - BETA_TWO) * hessian
+    update = jnp.clip(moment_new / (GAMMA_CLIP * curvature_next), -1.0, 1.0) * owned_mask
+    return update, curvature_next * owned_mask
 
 
 def solution(mesh):

time: 97.2 us -> 89.6 us (0.922)
  local copies, waits for them, and re-layouts: 9.47 us -> 1.5 us
  other arithmetic: 0 us -> 1.79 us
  Pallas kernels: 86.1 us -> 84.7 us
    unnamed x4 -> x9, local copies, waits for them, and re-layouts: 6.66 us -> 1.07 us
    while x2 -> x0, local copies, waits for them, and re-layouts: 1.55 us -> none
    pallas_call x2, Pallas kernels: 86.1 us -> 84.7 us  [the longest x1 83.5 us: round_step(): pl.pallas_call(kernel, out_shape=jax.ShapeDtypeStruct((2, 2 * BLOCK, 2 *...]
    slice x1 -> x0, local copies, waits for them, and re-layouts: 1.22 us -> none  [step(): return (round_ + 1, table[ROUNDS_AT, 0], update, new_curvature, sums)]
where the time goes in v4:
time: 89.6 us; the launch traced here: 89.4 us
  Pallas kernels  84.7 us (95%)
  other arithmetic  1.79 us (2%)
  local copies, waits for them, and re-layouts  1.5 us (2%)
    pallas_call x1, Pallas kernels, round_step(): pl.pallas_call(kernel, out_shape=jax.ShapeDtypeStruct((2, 2 * BLOCK, 2 *...  83.5 us

profile of v4, /device:TPU:5, one launch (start us, length us, event | category | flops | bytes accessed | tf_op | source)
XLA Modules:
  0.0 89.4 jit_solution(9781132963737243576)
XLA Ops:
  0.6 0.0 copy-start.1
  0.6 0.0 copy-start
  0.7 0.8 dynamic-slice_convert_fusion
  1.5 0.1 copy.10
  1.6 0.8 copy.8.mask_ref
  2.4 1.1 %tables.2 = (s32[24,128]{1,0:T(8,128)}, s32[1]{0:T(128)}) custom-call(s32[1]{0:T(128)} %constant.7.clone.1.round_ref, s32[64,8]{1,0:T(8,128)S(1)} %copy.8.mask_ref), custom_call_target="tpu_custom_call" | custom-call | tf_op jit(solution)/shard_map/tables/pallas_call | solution.py:451
  3.5 0.3 broadcast_in_dim.7
  3.9 83.5 %round_step.2 = f32[2,256,256]{2,1,0:T(8,128)S(1)} custom-call(s32[24,128]{1,0:T(8,128)} %get-tuple-element.43.refs_0_, bf16[1024,2048]{1,0:T(8,128)(2,1)} %refs_1_.1, bf16[1024,256]{1,0:T(8,128)(2,1)} %refs_2_.1, bf16[1024,256]{1,0:T(8,128)(2,1)} %refs_3_.1), custom_call_target="tpu_custom_call" | custom-call | tf_op jit(solution)/shard_map/round_step/pallas_call | solution.py:377
  87.4 0.0 copy-done.1
  87.4 0.0 copy-done
  87.4 0.0 copy-start.2
  87.4 0.0 copy-start.3
  87.5 0.7 while.10
  88.2 0.2 copy-done.2
  88.4 0.1 copy-done.3
  88.5 0.9 %bitcast_multiply_fusion = (f32[256,256]{1,0:T(8,128)}, f32[256,256]{1,0:T(8,128)}) fusion(f32[32,8,2,128]{3,2,1,0:T(2,128)S(1)} %bitcast.28, f32[2,256,256]{2,1,0:T(8,128)S(1)} %broadcast_multiply_fusion, f32[256,256]{1,0:T(8,128)S(1)} %copy-done.2, f32[256,256]{1,0:T(8,128)S(1)} %copy-done.3), kind=kLoop, calls=%fused_computation.3 | loop fusion | flops 851968 | bytes 1835008 | tf_op jit(solution)/shard_map/mul | solution.py:482
  (2 shorter events, 0.0 us)
Async XLA Ops:
  0.6 86.8 %copy-start.1 = (bf16[1024,256]{1,0:T(8,128)(2,1)S(1)}, bf16[1024,256]{1,0:T(8,128)(2,1)}, u32[]{:S(2)}) copy-start(bf16[1024,256]{1,0:T(8,128)(2,1)} %refs_3_.1) | copy-start | bytes 1572868
  0.6 86.8 %copy-start = (bf16[1024,256]{1,0:T(8,128)(2,1)S(1)}, bf16[1024,256]{1,0:T(8,128)(2,1)}, u32[]{:S(2)}) copy-start(bf16[1024,256]{1,0:T(8,128)(2,1)} %refs_2_.1) | copy-start | bytes 1572868
  87.4 1.0 %copy-start.2 = (f32[256,256]{1,0:T(8,128)S(1)}, f32[256,256]{1,0:T(8,128)}, u32[]{:S(2)}) copy-start(f32[256,256]{1,0:T(8,128)} %param.13) | copy-start | bytes 786436
  87.4 1.0 %copy-start.3 = (f32[256,256]{1,0:T(8,128)S(1)}, f32[256,256]{1,0:T(8,128)}, u32[]{:S(2)}) copy-start(f32[256,256]{1,0:T(8,128)} %param.12) | copy-start | bytes 786436

commit v5 on v4

--- a/solution.py
+++ b/solution.py
@@ -19,6 +19,9 @@
 WAVES = ((0, 0, 14), (0, 14, 12), (1, 0, 16), (2, 0, 16))
 GROUP_SLOTS = tuple(sum(n for g, _, n in WAVES if g == group) for group in range(3))
 TILE_ROWS = 16
+CHUNKS = (((0, 8),), ((0, 8),), ((0, 4), (4, 2), (6, 2)))
+FAR_PIECES = tuple((cc, c, g) for cc in range(2) for c in range(len(CHUNKS[1 + cc])) for g in range(2))
+NO_TILE = 3e38
 
 FIRST_COL = (0, 4, 6)
 LIST_AT = TILE_ROWS
@@ -40,12 +43,13 @@
         landed=pltpu.VMEM((32, 2, 2, 8, BLOCK), F32),
         in_sem=dma((5,)),
         pair_send=dma((4,)), pair_recv=dma((4,)),
-        far_send=dma((4,)), far_recv=dma((4,)),
-        fwd_send=dma((4,)), fwd_recv=dma((4,)),
+        far_send=dma((len(FAR_PIECES),)), far_recv=dma((len(FAR_PIECES),)),
+        fwd_send=dma((len(FAR_PIECES),)), fwd_recv=dma((len(FAR_PIECES),)),
     )
     for g, cols in enumerate(GROUP_COLS):
         n = GROUP_SLOTS[g]
-        shapes[f"cots{g}"] = pltpu.VMEM((cols, tokens, 2 * BLOCK), BF16)
+        for c, (_, eighths) in enumerate(CHUNKS[g]):
+            shapes[f"cots{g}_{c}"] = pltpu.VMEM((cols, eighths * tokens // 8, 2 * BLOCK), BF16)
         shapes[f"tiles{g}"] = pltpu.VMEM((n + 1, 8, BLOCK), F32)
         per_owner = (2, 2) if g == 0 else (2,)
         shapes[f"dense{g}"] = pltpu.VMEM((16, *per_owner, 8, BLOCK), F32)
@@ -104,18 +108,23 @@
     lax.fori_loop(0, 32, greet, 0)
     pl.semaphore_wait(barrier, jnp.where(m == x, 38, 39))
 
-    def own(cc, g):
-        return (true_ref, sampled_ref)[g].at[:, pl.ds(cc * BLOCK, BLOCK)]
+    eighth = true_ref.shape[0] // 8
+
+    def own(cc, g, first=0, count=8):
+        return (true_ref, sampled_ref)[g].at[pl.ds(first * eighth, count * eighth), lanes(cc)]
 
     def lanes(g):
         return pl.ds(g * BLOCK, BLOCK)
 
-    pieces = [(cc, g) for cc in range(2) for g in range(2)]
-    inputs, pairs, fars, fwds, started = [], [], [], [], []
-    for i, (cc, g) in enumerate(pieces):
-        near_place = r["cots0"].at[core * 2 + cc, :, lanes(g)]
-        far_place = r[f"cots{1 + cc}"].at[core, :, lanes(g)]
-        fars.append(remote(own(cc, g), far_place, r["far_send"].at[i], r["far_recv"].at[i], far))
+    def far_place(cc, c, g):
+        return r[f"cots{1 + cc}_{c}"].at[core, :, lanes(g)]
+
+    inputs, pairs, fars, fwds, started = [], [], [], {}, []
+    for i, (cc, c, g) in enumerate(FAR_PIECES):
+        piece = own(cc, g, *CHUNKS[1 + cc][c])
+        fars.append(remote(piece, far_place(cc, c, g), r["far_send"].at[i], r["far_recv"].at[i], far))
+    for i, (cc, g) in enumerate((cc, g) for cc in range(2) for g in range(2)):
+        near_place = r["cots0_0"].at[core * 2 + cc, :, lanes(g)]
         pairs.append(remote(own(cc, g), near_place, r["pair_send"].at[i], r["pair_recv"].at[i], pair))
         inputs.append(pltpu.make_async_copy(own(cc, g), near_place, r["in_sem"].at[1 + i]))
     for copies in (fars, pairs, inputs):
@@ -129,18 +138,21 @@
 
     lax.fori_loop(0, TILE_ROWS, transpose, 0)
 
-    def products(w):
+    def products(w, c=0):
         group, first, n = WAVES[w]
-        cots, part = r[f"cots{group}"], r[f"part{w}"]
+        cots, part = r[f"cots{group}_{c}"], r[f"part{w}"]
+        start, count = CHUNKS[group][c]
 
         def one(i, carry):
             for u in range(2):
                 s = 2 * i + u
                 row = table_ref[LIST_AT + 2 * group, first + s]
                 col = table_ref[LIST_AT + 2 * group + 1, first + s]
-                tile = jnp.dot(r["acts_t"][row], cots[col], preferred_element_type=F32)
+                strip = r["acts_t"][row][:, start * eighth : (start + count) * eighth]
+                tile = jnp.dot(strip, cots[col], preferred_element_type=F32)
                 for g in range(2):
-                    part[g, :, s] = tile[:, g * BLOCK : (g + 1) * BLOCK].reshape(16, 8, BLOCK)
+                    term = tile[:, g * BLOCK : (g + 1) * BLOCK].reshape(16, 8, BLOCK)
+                    part[g, :, s] = term if c == 0 else part[g, :, s] + term
             return carry
 
         lax.fori_loop(0, n // 2, one, 0)
@@ -253,7 +265,7 @@
             if group == g:
                 swaps[w].wait_recv()
                 tiles[pl.ds(first, n)] = r[f"last{w}"][h] + r[f"over{w}"][...]
-        tiles[GROUP_SLOTS[g]] = jnp.zeros((8, BLOCK), F32)
+        tiles[GROUP_SLOTS[g]] = jnp.full((8, BLOCK), NO_TILE, F32)
 
         def one(t, carry):
             core_to = lax.rem(t, 2)
@@ -287,18 +299,18 @@
 
         lax.fori_loop(0, 16, one, 0)
 
-    def forward(cc):
-        for i, (piece_cc, g) in enumerate(pieces):
-            if piece_cc == cc:
+    def forward(cc, c=0):
+        for i, piece in enumerate(FAR_PIECES):
+            if piece[:2] == (cc, c):
                 fars[i].wait_recv()
-                place = r[f"cots{1 + cc}"].at[core, :, lanes(g)]
-                copy = remote(place, place, r["fwd_send"].at[i], r["fwd_recv"].at[i], pair)
-                copy.start()
-                fwds.append(copy)
-
-    def forwarded(cc):
-        for copy in fwds[cc * 2 : cc * 2 + 2]:
-            copy.wait_recv()
+                place = far_place(*piece)
+                fwds[piece] = remote(place, place, r["fwd_send"].at[i], r["fwd_recv"].at[i], pair)
+                fwds[piece].start()
+
+    def forwarded(cc, c=0):
+        for piece in FAR_PIECES:
+            if piece[:2] == (cc, c):
+                fwds[piece].wait_recv()
 
     for copy in inputs:
         copy.wait()
@@ -315,11 +327,17 @@
     products(2)
     open_first(2)
     close_first(0)
+    forward(1, 0)
     close_first(1)
+    forwarded(1, 0)
+    products(3, 0)
+    forward(1, 1)
+    forwarded(1, 1)
+    products(3, 1)
     turn_first(2)
-    forward(1)
-    forwarded(1)
-    products(3)
+    forward(1, 2)
+    forwarded(1, 2)
+    products(3, 2)
     open_first(3)
     turn_second(0)
     turn_second(1)
@@ -328,11 +346,11 @@
     close_first(2)
     turn_first(3)
     turn_second(2)
-    deliver(0)
     close_second(2)
     close_first(3)
+    turn_second(3)
+    deliver(0)
     deliver(1)
-    turn_second(3)
     close_second(3)
     deliver(2)
 
@@ -365,7 +383,7 @@
 
     lax.fori_loop(0, 16, finish, 0)
 
-    for copy in (*fars, *pairs, *fwds, *started):
+    for copy in (*fars, *pairs, *fwds.values(), *started):
         copy.wait_send()
     for g in range(3):
         drain(g)
@@ -458,8 +476,6 @@
 
 
 def on_device(activations, cot_true, cot_sampled, tile_mask, moment, curvature):
-    m = lax.axis_index("mp")
-    dp = lax.axis_index("dp")
     tokens_all = activations.shape[0] * lax.axis_size("dp")
 
     def one_round(round_):
@@ -467,19 +483,18 @@
         return round_step(table, activations, cot_true, cot_sampled), rounds
 
     sums, rounds = one_round(jnp.int32(0))
-    _, sums = lax.while_loop(
-        lambda state: state[0] < rounds[0],
-        lambda state: (state[0] + 1, state[1] + one_round(state[0])[0]),
-        (jnp.int32(1), sums),
-    )
-    owned = lax.dynamic_slice(tile_mask, (dp * 2, m * 2), (2, 2))
-    owned_mask = jnp.repeat(jnp.repeat(owned, BLOCK, axis=0), BLOCK, axis=1).astype(F32)
+    def again(state):
+        found, _ = one_round(state[0])
+        return state[0] + 1, jnp.where(found < NO_TILE / 2, found, state[1])
+
+    _, sums = lax.while_loop(lambda state: state[0] < rounds[0], again, (jnp.int32(1), sums))
+    kept = sums[0] < NO_TILE / 2
     grads = sums * (1.0 / tokens_all)
     moment_new = BETA_ONE * moment + (1.0 - BETA_ONE) * grads[0]
     hessian = tokens_all * grads[1] * grads[1]
     curvature_next = BETA_TWO * curvature + (1.0 - BETA_TWO) * hessian
-    update = jnp.clip(moment_new / (GAMMA_CLIP * curvature_next), -1.0, 1.0) * owned_mask
-    return update, curvature_next * owned_mask
+    update = jnp.clip(moment_new / (GAMMA_CLIP * curvature_next), -1.0, 1.0)
+    return jnp.where(kept, update, 0.0), jnp.where(kept, curvature_next, 0.0)
 
 
 def solution(mesh):

time: 89.6 us -> 87.9 us (0.981)
  Pallas kernels: 84.7 us -> 83.6 us
    select_n x0 -> x2, other arithmetic: none -> 1.64 us  [on_device(): return (jnp.where(kept, update, 0.0), jnp.where(kept, curvature_next, 0.0))]
    pallas_call x1, Pallas kernels: 83.5 us -> 82.5 us  [round_step(): pl.pallas_call(kernel, out_shape=jax.ShapeDtypeStruct((2, 2 * BLOCK, 2 *...]
    mul x1 -> x0, other arithmetic: 0.91 us -> none  [on_device(): return (update, curvature_next * owned_mask)]
where the time goes in v5:
time: 87.9 us; the launch traced here: 87.7 us
  Pallas kernels  83.6 us (95%)
  other arithmetic  1.67 us (2%)
  local copies, waits for them, and re-layouts  1.08 us (1%)
    pallas_call x1, Pallas kernels, round_step(): pl.pallas_call(kernel, out_shape=jax.ShapeDtypeStruct((2, 2 * BLOCK, 2 *...  82.5 us

profile of v5, /device:TPU:5, one launch (start us, length us, event | category | flops | bytes accessed | tf_op | source)
XLA Modules:
  0.0 87.7 jit_solution(6110129290700337300)
XLA Ops:
  0.6 0.0 copy-start.1
  0.6 0.0 copy-start
  0.7 0.9 copy.8.mask_ref
  1.5 1.1 %tables.2 = (s32[24,128]{1,0:T(8,128)}, s32[1]{0:T(128)}) custom-call(s32[1]{0:T(128)} %constant.1.clone.1.round_ref, s32[64,8]{1,0:T(8,128)S(1)} %copy.8.mask_ref), custom_call_target="tpu_custom_call" | custom-call | tf_op jit(solution)/shard_map/tables/pallas_call | solution.py:469
  2.7 82.5 %round_step.2 = f32[2,256,256]{2,1,0:T(8,128)S(1)} custom-call(s32[24,128]{1,0:T(8,128)} %get-tuple-element.43.refs_0_, bf16[1024,2048]{1,0:T(8,128)(2,1)} %refs_1_.1, bf16[1024,256]{1,0:T(8,128)(2,1)} %refs_2_.1, bf16[1024,256]{1,0:T(8,128)(2,1)} %refs_3_.1), custom_call_target="tpu_custom_call" | custom-call | tf_op jit(solution)/shard_map/round_step/pallas_call | solution.py:395
  85.1 0.0 copy-done.1
  85.1 0.0 copy-done
  85.1 0.0 copy-start.2
  85.1 0.0 copy-start.3
  85.2 0.7 while.10
  85.9 0.2 copy-done.2
  86.1 0.8 broadcast_select_fusion
  86.9 0.0 copy-done.3
  86.9 0.8 fusion.6
  (1 shorter events, 0.0 us)
Async XLA Ops:
  0.6 84.5 %copy-start.1 = (bf16[1024,256]{1,0:T(8,128)(2,1)S(1)}, bf16[1024,256]{1,0:T(8,128)(2,1)}, u32[]{:S(2)}) copy-start(bf16[1024,256]{1,0:T(8,128)(2,1)} %refs_3_.1) | copy-start | bytes 1572868
  0.6 84.5 %copy-start = (bf16[1024,256]{1,0:T(8,128)(2,1)S(1)}, bf16[1024,256]{1,0:T(8,128)(2,1)}, u32[]{:S(2)}) copy-start(bf16[1024,256]{1,0:T(8,128)(2,1)} %refs_2_.1) | copy-start | bytes 1572868
  85.1 1.0 %copy-start.2 = (f32[256,256]{1,0:T(8,128)S(1)}, f32[256,256]{1,0:T(8,128)}, u32[]{:S(2)}) copy-start(f32[256,256]{1,0:T(8,128)} %param.13) | copy-start | bytes 786436
  85.1 1.7 %copy-start.3 = (f32[256,256]{1,0:T(8,128)S(1)}, f32[256,256]{1,0:T(8,128)}, u32[]{:S(2)}) copy-start(f32[256,256]{1,0:T(8,128)} %param.12) | copy-start | bytes 786436

commit v6 on v5

--- a/solution.py
+++ b/solution.py
@@ -38,10 +38,13 @@
 def scratch_list(tokens):
     dma = pltpu.SemaphoreType.DMA
     shapes = dict(
+        mask=pltpu.VMEM((4 * TILE_ROWS, 8), I32),
+        table_made=pltpu.VMEM(TABLE, I32),
+        table=pltpu.SMEM(TABLE, I32),
         acts=pltpu.VMEM((tokens, TILE_ROWS * BLOCK), BF16),
         acts_t=pltpu.VMEM((TILE_ROWS, BLOCK, tokens), BF16),
         landed=pltpu.VMEM((32, 2, 2, 8, BLOCK), F32),
-        in_sem=dma((5,)),
+        in_sem=dma((7,)),
         pair_send=dma((4,)), pair_recv=dma((4,)),
         far_send=dma((len(FAR_PIECES),)), far_recv=dma((len(FAR_PIECES),)),
         fwd_send=dma((len(FAR_PIECES),)), fwd_recv=dma((len(FAR_PIECES),)),
@@ -72,11 +75,71 @@
     return shapes
 
 
+def make_table(m, round_ref, mask_ref, table_ref, rounds_ref):
+    half = m // 2
+    own = mask_ref[pl.ds(pl.multiple_of(m * TILE_ROWS, TILE_ROWS), TILE_ROWS), :]
+    kept_all = jnp.where(own > 0, 1, 0)
+    row_index = lax.broadcasted_iota(I32, (TILE_ROWS, 1), 0)
+    slot_index = lax.broadcasted_iota(I32, (TILE_ROWS, BLOCK), 1)
+    lane = lax.broadcasted_iota(I32, (TILE_ROWS, BLOCK), 1)
+    before_rows = lax.broadcasted_iota(I32, (TILE_ROWS, TILE_ROWS), 1) < lax.broadcasted_iota(
+        I32, (TILE_ROWS, TILE_ROWS), 0
+    )
+    place = jnp.zeros((TILE_ROWS, BLOCK), I32)
+    lines = []
+    for g, cols in enumerate(GROUP_COLS):
+        n = GROUP_SLOTS[g]
+        near, other = (
+            [half_ * 4 + k for k in range(4)] if g == 0 else [(1 - half_) * 4 + k * 2 + g - 1 for k in range(2)]
+            for half_ in range(2)
+        )
+        kept = [
+            jnp.where(half == 0, kept_all[:, near[k] : near[k] + 1], kept_all[:, other[k] : other[k] + 1])
+            for k in range(cols)
+        ]
+        per_row = functools.reduce(lambda p, q: p + q, kept)
+        turned = jnp.sum(
+            jnp.where(
+                lax.broadcasted_iota(I32, (TILE_ROWS, TILE_ROWS), 0)
+                == lax.broadcasted_iota(I32, (TILE_ROWS, TILE_ROWS), 1),
+                per_row, 0,
+            ),
+            axis=0, keepdims=True,
+        )
+        seen = jnp.sum(jnp.where(before_rows, turned, 0), axis=1, keepdims=True) - round_ref[0] * n
+        rows_line = jnp.zeros((1, BLOCK), I32)
+        cols_line = jnp.zeros((1, BLOCK), I32)
+        for k in range(cols):
+            here = (kept[k] > 0) & (seen >= 0) & (seen < n)
+            place = jnp.where(lane == FIRST_COL[g] + k, jnp.where(here, seen, n), place)
+            chosen = jnp.where(here, seen, -1) == slot_index
+            rows_line = rows_line + jnp.sum(jnp.where(chosen, row_index, 0), axis=0, keepdims=True)
+            cols_line = cols_line + jnp.sum(jnp.where(chosen, k, 0), axis=0, keepdims=True)
+            seen = seen + kept[k]
+        lines += [rows_line, cols_line]
+
+    counts = jnp.sum(jnp.where(mask_ref[...] > 0, 1, 0).reshape(4, TILE_ROWS, 8), axis=1)
+    source = lax.broadcasted_iota(I32, (4, 8), 0)
+    column = lax.broadcasted_iota(I32, (4, 8), 1)
+    near = (source // 2) == (column // 4)
+    even = lax.rem(column, 2) == 0
+    needed = jnp.zeros((4, 1), I32)
+    for g, inside in enumerate((near, ~near & even, ~near & ~even)):
+        filled = jnp.sum(jnp.where(inside, counts, 0), axis=1, keepdims=True)
+        rounds = sum(jnp.where(filled > n * GROUP_SLOTS[g], 1, 0) for n in range(TILE_ROWS * GROUP_COLS[g] // GROUP_SLOTS[g] + 1))
+        needed = jnp.maximum(needed, rounds)
+    rounds_ref[0] = jnp.max(needed)
+    lines.append(jnp.zeros((2, BLOCK), I32))
+    table_ref[pl.ds(0, TILE_ROWS)] = place
+    table_ref[pl.ds(TILE_ROWS, 8)] = jnp.concatenate(lines, axis=0)
+
+
 def kernel(*refs):
     refs = list(refs)
     names = list(scratch_list(8))
     r = dict(zip(names, refs[-len(names):]))
-    table_ref, acts_hbm, true_ref, sampled_ref, sums_ref = refs[: -len(names)]
+    round_ref, mask_hbm, acts_hbm, true_ref, sampled_ref, sums_ref, rounds_ref = refs[: -len(names)]
+    table_ref = r["table"]
 
     dp = lax.axis_index("dp")
     m = lax.axis_index("mp")
@@ -93,6 +156,8 @@
     across_h = device_at(x, z, 1 - h, m)
 
     acts_in = pltpu.make_async_copy(acts_hbm, r["acts"], r["in_sem"].at[0])
+    mask_in = pltpu.make_async_copy(mask_hbm, r["mask"], r["in_sem"].at[5])
+    mask_in.start()
     acts_in.start()
 
     barrier = pltpu.get_barrier_semaphore()
@@ -130,6 +195,10 @@
     for copies in (fars, pairs, inputs):
         for copy in copies:
             copy.start()
+    mask_in.wait()
+    make_table(m, round_ref, r["mask"], r["table_made"], rounds_ref)
+    table_in = pltpu.make_async_copy(r["table_made"], r["table"], r["in_sem"].at[6])
+    table_in.start()
     acts_in.wait()
 
     def transpose(row, carry):
@@ -312,6 +381,7 @@
             if piece[:2] == (cc, c):
                 fwds[piece].wait_recv()
 
+    table_in.wait()
     for copy in inputs:
         copy.wait()
     for copy in pairs:
@@ -394,10 +464,10 @@
     hbm = pl.BlockSpec(memory_space=pl.ANY)
     return pl.pallas_call(
         kernel,
-        out_shape=jax.ShapeDtypeStruct((2, 2 * BLOCK, 2 * BLOCK), F32),
-        in_specs=[smem, hbm, hbm, hbm],
-        out_specs=pl.BlockSpec(memory_space=pltpu.VMEM),
-        scratch_shapes=list(scratch_list(args[1].shape[0]).values()),
+        out_shape=(jax.ShapeDtypeStruct((2, 2 * BLOCK, 2 * BLOCK), F32), jax.ShapeDtypeStruct((1,), I32)),
+        in_specs=[smem, hbm, hbm, hbm, hbm],
+        out_specs=(pl.BlockSpec(memory_space=pltpu.VMEM), smem),
+        scratch_shapes=list(scratch_list(args[2].shape[0]).values()),
         compiler_params=pltpu.CompilerParams(
             collective_id=0, has_side_effects=True, vmem_limit_bytes=60 << 20
         ),
@@ -405,82 +475,11 @@
     )(*args)
 
 
-def table_kernel(round_ref, mask_ref, table_ref, rounds_ref):
-    m = lax.axis_index("mp")
-    half = m // 2
-    own = mask_ref[pl.ds(pl.multiple_of(m * TILE_ROWS, TILE_ROWS), TILE_ROWS), :]
-    kept_all = jnp.where(own > 0, 1, 0)
-    row_index = lax.broadcasted_iota(I32, (TILE_ROWS, 1), 0)
-    slot_index = lax.broadcasted_iota(I32, (TILE_ROWS, BLOCK), 1)
-    lane = lax.broadcasted_iota(I32, (TILE_ROWS, BLOCK), 1)
-    before_rows = lax.broadcasted_iota(I32, (TILE_ROWS, TILE_ROWS), 1) < lax.broadcasted_iota(
-        I32, (TILE_ROWS, TILE_ROWS), 0
-    )
-    place = jnp.zeros((TILE_ROWS, BLOCK), I32)
-    lines = []
-    for g, cols in enumerate(GROUP_COLS):
-        n = GROUP_SLOTS[g]
-        near, other = (
-            [half_ * 4 + k for k in range(4)] if g == 0 else [(1 - half_) * 4 + k * 2 + g - 1 for k in range(2)]
-            for half_ in range(2)
-        )
-        kept = [
-            jnp.where(half == 0, kept_all[:, near[k] : near[k] + 1], kept_all[:, other[k] : other[k] + 1])
-            for k in range(cols)
-        ]
-        per_row = functools.reduce(lambda p, q: p + q, kept)
-        turned = jnp.sum(
-            jnp.where(
-                lax.broadcasted_iota(I32, (TILE_ROWS, TILE_ROWS), 0)
-                == lax.broadcasted_iota(I32, (TILE_ROWS, TILE_ROWS), 1),
-                per_row, 0,
-            ),
-            axis=0, keepdims=True,
-        )
-        seen = jnp.sum(jnp.where(before_rows, turned, 0), axis=1, keepdims=True) - round_ref[0] * n
-        rows_line = jnp.zeros((1, BLOCK), I32)
-        cols_line = jnp.zeros((1, BLOCK), I32)
-        for k in range(cols):
-            here = (kept[k] > 0) & (seen >= 0) & (seen < n)
-            place = jnp.where(lane == FIRST_COL[g] + k, jnp.where(here, seen, n), place)
-            chosen = jnp.where(here, seen, -1) == slot_index
-            rows_line = rows_line + jnp.sum(jnp.where(chosen, row_index, 0), axis=0, keepdims=True)
-            cols_line = cols_line + jnp.sum(jnp.where(chosen, k, 0), axis=0, keepdims=True)
-            seen = seen + kept[k]
-        lines += [rows_line, cols_line]
-
-    counts = jnp.sum(jnp.where(mask_ref[...] > 0, 1, 0).reshape(4, TILE_ROWS, 8), axis=1)
-    source = lax.broadcasted_iota(I32, (4, 8), 0)
-    column = lax.broadcasted_iota(I32, (4, 8), 1)
-    near = (source // 2) == (column // 4)
-    even = lax.rem(column, 2) == 0
-    needed = jnp.zeros((4, 1), I32)
-    for g, inside in enumerate((near, ~near & even, ~near & ~even)):
-        filled = jnp.sum(jnp.where(inside, counts, 0), axis=1, keepdims=True)
-        rounds = sum(jnp.where(filled > n * GROUP_SLOTS[g], 1, 0) for n in range(TILE_ROWS * GROUP_COLS[g] // GROUP_SLOTS[g] + 1))
-        needed = jnp.maximum(needed, rounds)
-    rounds_ref[0] = jnp.max(needed)
-    lines.append(jnp.zeros((2, BLOCK), I32))
-    table_ref[pl.ds(0, TILE_ROWS)] = place
-    table_ref[pl.ds(TILE_ROWS, 8)] = jnp.concatenate(lines, axis=0)
-
-
-def table_of(tile_mask, round_):
-    return pl.pallas_call(
-        table_kernel,
-        out_shape=(jax.ShapeDtypeStruct(TABLE, I32), jax.ShapeDtypeStruct((1,), I32)),
-        in_specs=[pl.BlockSpec(memory_space=pltpu.SMEM), pl.BlockSpec(memory_space=pltpu.VMEM)],
-        out_specs=(pl.BlockSpec(memory_space=pltpu.VMEM), pl.BlockSpec(memory_space=pltpu.SMEM)),
-        name="tables",
-    )(round_.reshape(1), tile_mask)
-
-
 def on_device(activations, cot_true, cot_sampled, tile_mask, moment, curvature):
     tokens_all = activations.shape[0] * lax.axis_size("dp")
 
     def one_round(round_):
-        table, rounds = table_of(tile_mask, round_)
-        return round_step(table, activations, cot_true, cot_sampled), rounds
+        return round_step(round_.reshape(1), tile_mask, activations, cot_true, cot_sampled)
 
     sums, rounds = one_round(jnp.int32(0))
     def again(state):

time: 87.9 us -> 86.6 us (0.985); the launches traced: 87.7 us -> 85.5 us
  Pallas kernels: 83.6 us -> 81.3 us
    pallas_call x2 -> x1, Pallas kernels: 83.6 us -> 81.3 us  [round_step(): pl.pallas_call(kernel, out_shape=(jax.ShapeDtypeStruct((2, 2 * BLOCK, 2 *...]
where the time goes in v6:
time: 86.6 us; the launch traced here: 85.5 us
  Pallas kernels  81.3 us (94%)
  other arithmetic  1.67 us (2%)
  local copies, waits for them, and re-layouts  1.08 us (1%)
    pallas_call x1, Pallas kernels, round_step(): pl.pallas_call(kernel, out_shape=(jax.ShapeDtypeStruct((2, 2 * BLOCK, 2 *...  81.3 us

profile of v6, /device:TPU:5, one launch (start us, length us, event | category | flops | bytes accessed | tf_op | source)
XLA Modules:
  0.0 85.5 jit_solution(17497307587013379183)
XLA Ops:
  0.6 0.0 copy-start.1
  0.6 0.0 copy-start
  0.7 0.9 %copy.8.refs_1_ = s32[64,8]{1,0:T(8,128)S(1)} copy(s32[64,8]{0,1:T(8,128)} %param.11) | data formatting | bytes 4096 | tf_op args[3]
  1.5 81.3 %round_step.2 = (f32[2,256,256]{2,1,0:T(8,128)S(1)}, s32[1]{0:T(128)}) custom-call(s32[1]{0:T(128)} %constant.1.clone.1.refs_0_, s32[64,8]{1,0:T(8,128)S(1)} %copy.8.refs_1_, bf16[1024,2048]{1,0:T(8,128)(2,1)} %refs_2_.1, bf16[1024,256]{1,0:T(8,128)(2,1)} %refs_3_.1, bf16[1024,256]{1,0:T(8,128)(2,1)} %refs_4_.1), custom_call_target="tpu_custom_call" | custom-call | tf_op jit(solution)/shard_map/round_step/pallas_call | solution.py:465
  82.9 0.0 copy-done.1
  82.9 0.0 copy-done
  82.9 0.0 copy-start.2
  82.9 0.0 copy-start.3
  82.9 0.7 while.10
  83.6 0.2 copy-done.2
  83.8 0.8 broadcast_select_fusion
  84.6 0.0 copy-done.3
  84.6 0.8 fusion.6
  (1 shorter events, 0.0 us)
Async XLA Ops:
  0.6 82.2 %copy-start.1 = (bf16[1024,256]{1,0:T(8,128)(2,1)S(1)}, bf16[1024,256]{1,0:T(8,128)(2,1)}, u32[]{:S(2)}) copy-start(bf16[1024,256]{1,0:T(8,128)(2,1)} %refs_4_.1) | copy-start | bytes 1572868
  0.6 82.2 %copy-start = (bf16[1024,256]{1,0:T(8,128)(2,1)S(1)}, bf16[1024,256]{1,0:T(8,128)(2,1)}, u32[]{:S(2)}) copy-start(bf16[1024,256]{1,0:T(8,128)(2,1)} %refs_3_.1) | copy-start | bytes 1572868
  82.9 1.0 %copy-start.2 = (f32[256,256]{1,0:T(8,128)S(1)}, f32[256,256]{1,0:T(8,128)}, u32[]{:S(2)}) copy-start(f32[256,256]{1,0:T(8,128)} %param.13) | copy-start | bytes 786436
  82.9 1.7 %copy-start.3 = (f32[256,256]{1,0:T(8,128)S(1)}, f32[256,256]{1,0:T(8,128)}, u32[]{:S(2)}) copy-start(f32[256,256]{1,0:T(8,128)} %param.12) | copy-start | bytes 786436

commit v7 on v6

--- a/solution.py
+++ b/solution.py
@@ -164,14 +164,7 @@
     for other in (pair, far, *along_x, *along_z, across_h):
         pl.semaphore_signal(barrier, inc=1, device_id=other, device_id_type=MESH)
 
-    def greet(sender, carry):
-        @pl.when(jnp.logical_not(jnp.logical_and(sender == dp, m == x)))
-        def _():
-            pl.semaphore_signal(barrier, inc=1, device_id=(sender, x), device_id_type=MESH)
-        return carry
-
-    lax.fori_loop(0, 32, greet, 0)
-    pl.semaphore_wait(barrier, jnp.where(m == x, 38, 39))
+    pl.semaphore_wait(barrier, 7)
 
     eighth = true_ref.shape[0] // 8
 

time: 86.6 us -> 83.2 us (0.961); the launches traced: 85.5 us -> 83 us
  Pallas kernels: 81.3 us -> 78.9 us
    pallas_call x1, Pallas kernels: 81.3 us -> 78.9 us  [round_step(): pl.pallas_call(kernel, out_shape=(jax.ShapeDtypeStruct((2, 2 * BLOCK, 2 *...]
where the time goes in v7:
time: 83.2 us; the launch traced here: 83 us
  Pallas kernels  78.9 us (95%)
  other arithmetic  1.67 us (2%)
  local copies, waits for them, and re-layouts  1.08 us (1%)
    pallas_call x1, Pallas kernels, round_step(): pl.pallas_call(kernel, out_shape=(jax.ShapeDtypeStruct((2, 2 * BLOCK, 2 *...  78.9 us

profile of v7, /device:TPU:5, one launch (start us, length us, event | category | flops | bytes accessed | tf_op | source)
XLA Modules:
  0.0 83.0 jit_solution(1084087696698465879)
XLA Ops:
  0.6 0.0 copy-start.1
  0.6 0.0 copy-start
  0.7 0.9 %copy.8.refs_1_ = s32[64,8]{1,0:T(8,128)S(1)} copy(s32[64,8]{0,1:T(8,128)} %param.11) | data formatting | bytes 4096 | tf_op args[3]
  1.5 78.9 %round_step.2 = (f32[2,256,256]{2,1,0:T(8,128)S(1)}, s32[1]{0:T(128)}) custom-call(s32[1]{0:T(128)} %constant.1.clone.1.refs_0_, s32[64,8]{1,0:T(8,128)S(1)} %copy.8.refs_1_, bf16[1024,2048]{1,0:T(8,128)(2,1)} %refs_2_.1, bf16[1024,256]{1,0:T(8,128)(2,1)} %refs_3_.1, bf16[1024,256]{1,0:T(8,128)(2,1)} %refs_4_.1), custom_call_target="tpu_custom_call" | custom-call | tf_op jit(solution)/shard_map/round_step/pallas_call | solution.py:458
  80.4 0.0 copy-done.1
  80.4 0.0 copy-done
  80.4 0.0 copy-start.2
  80.4 0.0 copy-start.3
  80.4 0.7 while.10
  81.2 0.2 copy-done.2
  81.4 0.8 broadcast_select_fusion
  82.2 0.0 copy-done.3
  82.2 0.8 %fusion.6 = f32[256,256]{1,0:T(8,128)} fusion(pred[256,256]{1,0:T(8,128)(4,1)S(1)} %get-tuple-element.68, f32[2,256,256]{2,1,0:T(8,128)S(1)} %broadcast_multiply_fusion, f32[256,256]{1,0:T(8,128)S(1)} %copy-done.3, f32[256,256]{1,0:T(8,128)S(1)} %copy-done.2), kind=kLoop, calls=%fused_computation.10 | loop fusion | flops 786432 | bytes 1376256 | tf_op jit(solution)/shard_map/jit(_where)/select_n | solution.py:489
  (1 shorter events, 0.0 us)
Async XLA Ops:
  0.6 79.8 %copy-start.1 = (bf16[1024,256]{1,0:T(8,128)(2,1)S(1)}, bf16[1024,256]{1,0:T(8,128)(2,1)}, u32[]{:S(2)}) copy-start(bf16[1024,256]{1,0:T(8,128)(2,1)} %refs_4_.1) | copy-start | bytes 1572868
  0.6 79.8 %copy-start = (bf16[1024,256]{1,0:T(8,128)(2,1)S(1)}, bf16[1024,256]{1,0:T(8,128)(2,1)}, u32[]{:S(2)}) copy-start(bf16[1024,256]{1,0:T(8,128)(2,1)} %refs_3_.1) | copy-start | bytes 1572868
  80.4 1.0 %copy-start.2 = (f32[256,256]{1,0:T(8,128)S(1)}, f32[256,256]{1,0:T(8,128)}, u32[]{:S(2)}) copy-start(f32[256,256]{1,0:T(8,128)} %param.13) | copy-start | bytes 786436
  80.4 1.7 %copy-start.3 = (f32[256,256]{1,0:T(8,128)S(1)}, f32[256,256]{1,0:T(8,128)}, u32[]{:S(2)}) copy-start(f32[256,256]{1,0:T(8,128)} %param.12) | copy-start | bytes 786436
